TPU v7x, 32 devices: a whole 2x2x4 slice. The times are simulated.
32 devices in a mesh: row: 8 (over z, x), col: 4 (over y, core).
Axes of the slice: x: 2, y: 2, z: 4, core: 2. Of those that a mesh axis runs over, the one named last changes fastest.
Arguments:
- tmatrix: bfloat16 [10656, 10656], P('row', 'col'), may hold values from -0.0625 to 0.0625
- panel: bfloat16 [10656, 2048], P('col', 'row'), may hold values from -6 to 6
- contrast: float32 [3, 144, 288], replicated, may hold values from -1.5 to 1.5
Outputs:
- excitation: bfloat16 [10656, 2048], P('col', 'row')
All inputs are finite; a program needn't handle non-finite values.
Results may differ from a plain program's by a relative error of at most 0.006.
Values may be sent and summed in bfloat16 or wider, within the bound.
No kernel may reach another device: no remote copies, remote signals or barrier semaphores. Data moves between devices by JAX's collectives and lax.ppermute only.
A program may use at most 192 MiB of HBM per device.

v0:
```python
import jax
import jax.numpy as jnp
import numpy as np
from jax import lax
from jax.sharding import PartitionSpec as P

LDEG = 72
ITERS = 2


def angular_tables(degree):
    lat_count = 2 * degree
    lon_count = 4 * degree
    freq_count = 2 * degree + 1
    colatitude = (np.arange(lat_count) + 0.5) * np.pi / lat_count
    cos_col = np.cos(colatitude)
    sin_col = np.sin(colatitude)
    legendre = np.zeros((freq_count, degree, lat_count))
    diagonal_term = np.full(lat_count, np.sqrt(0.5))
    for order_m in range(degree + 1):
        if order_m > 0:
            diagonal_term = (
                diagonal_term * np.sqrt((2.0 * order_m + 1.0) / (2.0 * order_m)) * sin_col
            )
        earlier = np.zeros(lat_count)
        latest = diagonal_term
        for degree_l in range(order_m, degree + 1):
            if degree_l == order_m:
                current = diagonal_term
            elif degree_l == order_m + 1:
                current = np.sqrt(2.0 * order_m + 3.0) * cos_col * diagonal_term
            else:
                factor_a = np.sqrt((4.0 * degree_l**2 - 1.0) / (degree_l**2 - order_m**2))
                factor_b = np.sqrt(
                    ((degree_l - 1.0) ** 2 - order_m**2) / (4.0 * (degree_l - 1.0) ** 2 - 1.0)
                )
                current = factor_a * (cos_col * latest - factor_b * earlier)
            if degree_l > order_m:
                earlier, latest = (latest, current)
            if degree_l >= 1:
                legendre[order_m, degree_l - 1] = current
                if order_m >= 1:
                    legendre[degree + order_m, degree_l - 1] = current
    longitude = 2.0 * np.pi * np.arange(lon_count) / lon_count
    fourier = np.zeros((freq_count, lon_count))
    fourier[0] = 1.0 / np.sqrt(2.0 * np.pi)
    for order_m in range(1, degree + 1):
        fourier[order_m] = np.cos(order_m * longitude) / np.sqrt(np.pi)
        fourier[degree + order_m] = np.sin(order_m * longitude) / np.sqrt(np.pi)
    weight = sin_col * (np.pi / lat_count) * (2.0 * np.pi / lon_count)
    return (legendre, fourier, weight)


def level_skips(degree):
    skips = []
    for freq_index in range(2 * degree + 1):
        order_m = freq_index if freq_index <= degree else freq_index - degree
        skips.append(max(order_m - 1, 0))
    return skips


def spread_levels(halves, degree):
    columns = halves.shape[2]
    pieces = []
    start = 0
    for skip in level_skips(degree):
        count = degree - skip
        if skip > 0:
            pieces.append(jnp.zeros((2, skip, columns), halves.dtype))
        pieces.append(halves[:, start : start + count, :])
        start = start + count
    return jnp.concatenate(pieces, axis=1).reshape(2, 2 * degree + 1, degree, columns)


def pick_levels(projected, degree):
    pieces = []
    for freq_index, skip in enumerate(level_skips(degree)):
        pieces.append(projected[:, freq_index, skip:, :])
    return jnp.concatenate(pieces, axis=1)


def contrast_apply(coefficients, contrast, degree):
    legendre, fourier, weight = angular_tables(degree)
    legendre_wide = jnp.asarray(legendre, jnp.float32)
    legendre_narrow = jnp.asarray(legendre, jnp.bfloat16)
    fourier = jnp.asarray(fourier, jnp.float32)
    weight = jnp.asarray(weight, jnp.float32)
    columns = coefficients.shape[1]
    halves = coefficients.astype(jnp.bfloat16).reshape(2, -1, columns)
    padded = spread_levels(halves, degree)
    triple = lax.Precision.HIGH
    latitude = jnp.einsum(
        "qlt,cqlk->cktq", legendre_narrow, padded, preferred_element_type=jnp.float32
    )
    surface = jnp.einsum(
        "cktq,qp->cktp", latitude, fourier, precision=triple, preferred_element_type=jnp.float32
    )
    polar = contrast[0] * surface[0] + contrast[1] * surface[1]
    azimuth = contrast[1] * surface[0] + contrast[2] * surface[1]
    weighted = jnp.stack([polar, azimuth]) * weight[:, None]
    spectrum = jnp.einsum(
        "cktp,qp->cktq", weighted, fourier, precision=triple, preferred_element_type=jnp.float32
    )
    projected = jnp.einsum(
        "qlt,cktq->cqlk",
        legendre_wide,
        spectrum,
        precision=triple,
        preferred_element_type=jnp.float32,
    )
    picked = pick_levels(projected, degree)
    return picked.reshape(-1, columns).astype(jnp.bfloat16)


def body(tmatrix, panel, contrast):
    row_count = lax.axis_size("row")
    col_count = lax.axis_size("col")
    per_device = panel.shape[1] // col_count
    local_rows = tmatrix.shape[0]
    current = panel
    for iteration in range(ITERS):
        partial_value = jnp.dot(
            tmatrix,
            lax.all_gather(current, "row", axis=1, tiled=True),
            preferred_element_type=jnp.float32,
        )
        grouped = partial_value.reshape(local_rows, row_count, col_count, per_device)
        summed = lax.psum_scatter(
            grouped.astype(jnp.bfloat16), "col", scatter_dimension=2, tiled=True
        )
        arrived = lax.all_to_all(summed, "row", split_axis=1, concat_axis=0, tiled=True)
        coupled = contrast_apply(
            arrived.reshape(arrived.shape[0], arrived.shape[3]), contrast, LDEG
        )
        full_rows = coupled.shape[0]
        returned = lax.all_to_all(
            coupled.reshape(col_count, full_rows // col_count, 1, per_device),
            "col",
            split_axis=0,
            concat_axis=2,
            tiled=True,
        )
        returned = returned.reshape(full_rows // col_count, col_count * per_device)
        current = (panel.astype(jnp.float32) + returned.astype(jnp.float32)).astype(jnp.bfloat16)
    return current


def solution(mesh):
    placed = (P("row", "col"), P("col", "row"), P())
    return jax.shard_map(
        body, mesh=mesh, in_specs=placed, out_specs=P("col", "row"), check_vma=False
    )
```

profile of v0, /device:TPU:0, one launch (start us, length us, event | category | flops | bytes accessed | tf_op | source)
XLA Modules:
  0.0 1476.1 jit_solution(9738215199244537752)
XLA Ops:
  7.3 160.5 %all-gather.3.cloned.1.call-done = bf16[2664,2048]{1,0:T(8,128)(2,1)} async-done(((bf16[2664,256]{1,0:T(8,128)(2,1)}), bf16[2664,2048]{1,0:T(8,128)(2,1)}) %all-gather.3.cloned.1.call-update) | async-done | bytes 10911760 | tf_op jit(solution)/shard_map/all_gather | solution.py:124
  167.9 21.4 %convolution_convert_fusion.1 = bf16[1332,2048]{1,0:T(8,128)(2,1)} fusion(bf16[1332,2664]{1,0:T(8,128)(2,1)} %param.11, bf16[2664,2048]{1,0:T(8,128)(2,1)} %all-gather.3.cloned.1.call-done), kind=kOutput, calls=%fused_computation.21 | convolution fusion | flops 14537170944 | bytes 23464512 | tf_op jit(solution)/shard_map/dot_general | solution.py:122
  189.3 8.2 copy.53
  198.7 108.2 %all-reduce.5.cloned.1.call-done = bf16[1332,8,4,64]{0,3,2,1:T(8,128)(2,1)} async-done(((bf16[1332,8,4,64]{0,3,2,1:T(8,128)(2,1)}), bf16[1332,8,4,64]{0,3,2,1:T(8,128)(2,1)}) %all-reduce.5.cloned.1.call-update) | async-done | bytes 5455888
  306.9 3.2 constant_dynamic-slice_fusion.1
  310.1 5.5 all-to-all-start
  316.4 33.1 %all-to-all-done = bf16[1332,8,1,64]{0,3,2,1:T(8,128)(2,1)S(1)} async-done(((bf16[1332,8,1,64]{0,3,2,1:T(8,128)(2,1)}), bf16[1332,8,1,64]{0,3,2,1:T(8,128)(2,1)S(1)}, u32[]{:S(2)}, u32[]{:S(2)}) %all-to-all-start) | async-done | bytes 1364000 | tf_op jit(solution)/shard_map/all_to_all | solution.py:131
  350.3 1.8 reshape_reshape.6
  407.0 5.4 concatenate.24
  426.7 55.6 %concatenate.23 = bf16[2,9417,64]{1,0,2:T(2,128)(2,1)} concatenate(bf16[2,144,64]{1,0,2:T(2,128)(2,1)S(1)} %slice.2639, bf16[2,1,64]{1,0,2:T(2,128)(2,1)S(1)} %broadcast.223, bf16[2,71,64]{1,0,2:T(2,128)(2,1)} %get-tuple-element.454, bf16[2,2,64]{1,0,2:T(2,128)(2,1)S(1)} %broadcast.224, bf16[2,70,64]{1,0,2:T(2,128)(2,1)} %get-tuple-element.452, ...), dimensions={1} | concatenate | bytes 4821504
  482.3 4.3 pad_maximum_fusion
  486.6 9.2 reshape.61
  495.8 13.2 convolution_bitcast_fusion.1
  509.0 39.7 %fusion.8 = f32[2,64,144,288]{3,2,1,0:T(8,128)} fusion(f32[145,288,1,1]{1,0,3,2:T(8,128)S(1)} %copy-done.6, f32[2,64,144,145]{2,1,0,3:T(8,128)} %convolution_bitcast_fusion.1), kind=kOutput, calls=%fused_computation.10 | convolution fusion | flops 4618321920 | bytes 32091264 | tf_op jit(solution)/shard_map/cktq,qp->cktp/dot_general | solution.py:95
  548.7 15.1 %multiply_add_fusion.3 = (f32[1,64,144,288]{3,2,1,0:T(8,128)S(1)}, f32[1,64,144,288]{3,2,1,0:T(8,128)}) fusion(f32[2,64,144,288]{3,2,1,0:T(8,128)} %fusion.8, f32[144,288]{1,0:T(8,128)} %get-tuple-element.457, f32[144,288]{1,0:T(8,128)S(1)} %get-tuple-element.455, f32[144,288]{1,0:T(8,128)S(1)} %get-tuple-element.456), kind=kLoop, calls=%fused_computation.17 | loop fusion | flops 15925248 | bytes 42964992 | tf_op jit(solution)/shard_map/add | solution.py:98
  563.9 20.4 %fusion = f32[2,64,144,145]{3,2,1,0:T(8,128)} fusion(f32[145,288,1,1]{1,0,3,2:T(8,128)} %constant.19, f32[1,64,144,288]{3,2,1,0:T(8,128)} %get-tuple-element.8, f32[1,64,144,288]{3,2,1,0:T(8,128)S(1)} %get-tuple-element.7, f32[144]{0:T(256)S(1)} %copy-done.84), kind=kOutput, calls=%fused_computation.1 | convolution fusion | flops 4628938752 | bytes 32091840 | tf_op jit(solution)/shard_map/cktp,qp->cktq/dot_general | solution.py:101
  584.3 22.2 %copy.58 = f32[2,64,144,145]{2,1,0,3:T(8,128)} copy(f32[2,64,144,145]{3,2,1,0:T(8,128)} %fusion) | data formatting | bytes 21381120 | tf_op jit(solution)/shard_map/cktp,qp->cktq/dot_general | solution.py:101
  606.4 14.8 %convert_bitcast_fusion.1 = bf16[2,145,72,64]{2,3,0,1:T(8,128)(2,1)} fusion(f32[2,64,144,145]{2,1,0,3:T(8,128)} %copy.58, f32[145,72,144,1]{2,1,3,0:T(8,128)} %constant.20), kind=kOutput, calls=%fused_computation.26 | convolution fusion | flops 1155916800 | bytes 19376640 | tf_op jit(solution)/shard_map/qlt,cktq->cqlk/dot_general | solution.py:104
  654.8 1.5 slice_bitcast_fusion.200
  660.7 1.5 slice_bitcast_fusion.204
  666.7 1.5 slice_bitcast_fusion.208
  669.7 1.5 slice_bitcast_fusion.210
  674.2 1.5 slice_bitcast_fusion.213
  677.2 1.5 slice_bitcast_fusion.215
  681.6 1.5 slice_bitcast_fusion.218
  683.1 1.5 slice_bitcast_fusion.148
  698.0 1.5 slice_bitcast_fusion.158
  701.0 1.5 slice_bitcast_fusion.160
  708.5 5.7 concatenate.17
  717.9 3.5 all-to-all-start.1
  721.5 1.8 copy.52
  723.3 16.0 %all-to-all-done.1 = bf16[4,2664,1,64]{1,3,2,0:T(8,128)(2,1)S(1)} async-done(((bf16[4,2664,1,64]{1,3,2,0:T(8,128)(2,1)}), bf16[4,2664,1,64]{1,3,2,0:T(8,128)(2,1)S(1)}, u32[]{:S(2)}, u32[]{:S(2)}) %all-to-all-start.1) | async-done | bytes 1364000 | tf_op jit(solution)/shard_map/all_to_all | solution.py:136
  741.0 155.1 %all-gather.5.cloned.1.call-done = bf16[2664,2048]{0,1:T(8,128)(2,1)} async-done(((bf16[2664,256]{0,1:T(8,128)(2,1)}), bf16[2664,2048]{0,1:T(8,128)(2,1)}) %all-gather.5.cloned.1.call-update) | async-done | bytes 10911760 | tf_op jit(solution)/shard_map/all_gather | solution.py:124
  896.1 21.5 %fusion.12 = bf16[1332,2048]{1,0:T(8,128)(2,1)} fusion(bf16[2664,2048]{0,1:T(8,128)(2,1)} %all-gather.5.cloned.1.call-done, bf16[1332,2664]{1,0:T(8,128)(2,1)} %param.11), kind=kOutput, calls=%fused_computation.22 | convolution fusion | flops 14537170944 | bytes 23464512 | tf_op jit(solution)/shard_map/dot_general | solution.py:122
  917.6 8.2 copy.63
  925.8 109.4 %all-reduce.7.cloned.1.call-done = bf16[1332,8,4,64]{0,3,2,1:T(8,128)(2,1)} async-done(((bf16[1332,8,4,64]{0,3,2,1:T(8,128)(2,1)}), bf16[1332,8,4,64]{0,3,2,1:T(8,128)(2,1)}) %all-reduce.7.cloned.1.call-update) | async-done | bytes 5455888
  1035.2 2.1 constant_dynamic-slice_fusion
  1037.3 39.5 %all_to_all.48 = bf16[1332,8,1,64]{0,3,2,1:T(8,128)(2,1)S(1)} all-to-all(bf16[1332,8,1,64]{0,3,2,1:T(8,128)(2,1)S(1)} %constant_dynamic-slice_fusion), channel_id=1, replica_groups=mesh['row'=8,'col'=4] {'row'}, dimensions={1} | all-to-all | bytes 2727936 | tf_op jit(solution)/shard_map/all_to_all | solution.py:131
  1077.6 1.8 reshape_reshape.7
  1133.9 4.7 concatenate.21
  1139.0 59.3 %concatenate.20 = bf16[2,9417,64]{1,0,2:T(2,128)(2,1)} concatenate(bf16[2,144,64]{1,0,2:T(2,128)(2,1)S(1)} %slice.2929, bf16[2,1,64]{1,0,2:T(2,128)(2,1)S(1)} %copy-done.9, bf16[2,71,64]{1,0,2:T(2,128)(2,1)} %get-tuple-element.342, bf16[2,2,64]{1,0,2:T(2,128)(2,1)S(1)} %copy-done.11, bf16[2,70,64]{1,0,2:T(2,128)(2,1)} %get-tuple-element.340, bf16[2,3,64]{1,0,2:T(2,128)(2,1)S(1)} %copy-done.13, ...), dimensions={1} | concatenate | bytes 4821504
  1198.3 4.3 pad_maximum_fusion.1
  1202.6 9.2 reshape.62
  1211.8 13.2 convolution_bitcast_fusion
  1225.0 39.5 %fusion.6 = f32[2,64,144,288]{3,2,1,0:T(8,128)} fusion(f32[145,288,1,1]{1,0,3,2:T(8,128)S(1)} %copy-done.7, f32[2,64,144,145]{2,1,0,3:T(8,128)} %convolution_bitcast_fusion), kind=kOutput, calls=%fused_computation.8 | convolution fusion | flops 4618321920 | bytes 32091264 | tf_op jit(solution)/shard_map/cktq,qp->cktp/dot_general | solution.py:95
  1264.6 15.1 %multiply_add_fusion.1 = (f32[1,64,144,288]{3,2,1,0:T(8,128)S(1)}, f32[1,64,144,288]{3,2,1,0:T(8,128)}) fusion(f32[2,64,144,288]{3,2,1,0:T(8,128)} %fusion.6, f32[144,288]{1,0:T(8,128)} %get-tuple-element.457, f32[144,288]{1,0:T(8,128)S(1)} %copy-done.3, f32[144,288]{1,0:T(8,128)S(1)} %copy-done.5), kind=kLoop, calls=%fused_computation.13 | loop fusion | flops 15925248 | bytes 42964992 | tf_op jit(solution)/shard_map/add | solution.py:98
  1279.7 20.4 %fusion.3 = f32[2,64,144,145]{3,2,1,0:T(8,128)} fusion(f32[145,288,1,1]{1,0,3,2:T(8,128)} %constant.19, f32[1,64,144,288]{3,2,1,0:T(8,128)} %get-tuple-element.6, f32[1,64,144,288]{3,2,1,0:T(8,128)S(1)} %get-tuple-element.5, f32[144]{0:T(256)S(1)} %copy-done.85), kind=kOutput, calls=%fused_computation.5 | convolution fusion | flops 4628938752 | bytes 32091840 | tf_op jit(solution)/shard_map/cktp,qp->cktq/dot_general | solution.py:101
  1300.1 22.2 %copy.68 = f32[2,64,144,145]{2,1,0,3:T(8,128)} copy(f32[2,64,144,145]{3,2,1,0:T(8,128)} %fusion.3) | data formatting | bytes 21381120 | tf_op jit(solution)/shard_map/cktp,qp->cktq/dot_general | solution.py:101
  1322.3 14.9 %convert_bitcast_fusion = bf16[2,145,72,64]{2,3,0,1:T(8,128)(2,1)} fusion(f32[2,64,144,145]{2,1,0,3:T(8,128)} %copy.68, f32[145,72,144,1]{2,1,3,0:T(8,128)} %constant.20), kind=kOutput, calls=%fused_computation.25 | convolution fusion | flops 1155916800 | bytes 19376640 | tf_op jit(solution)/shard_map/qlt,cktq->cqlk/dot_general | solution.py:104
  1364.9 1.5 slice_bitcast_fusion.35
  1367.9 1.5 slice_bitcast_fusion.37
  1375.4 1.5 slice_bitcast_fusion.42
  1376.9 1.5 slice_bitcast_fusion.43
  1379.8 1.5 slice_bitcast_fusion.45
  1388.8 1.5 slice_bitcast_fusion.51
  1391.8 1.5 slice_bitcast_fusion.53
  1394.7 1.5 slice_bitcast_fusion.55
  1396.2 1.5 slice_bitcast_fusion.56
  1400.7 1.5 slice_bitcast_fusion.59
  1402.2 1.5 slice_bitcast_fusion.60
  1406.7 1.5 slice_bitcast_fusion.63
  1438.4 5.7 concatenate.19
  1446.7 20.5 %all_to_all.49 = bf16[4,2664,1,64]{1,3,2,0:T(8,128)(2,1)S(1)} all-to-all(bf16[4,2664,1,64]{1,3,2,0:T(8,128)(2,1)S(1)} %copy.72), channel_id=1, replica_groups=mesh['row'=8,'col'=4] {'col'}, dimensions={0} | all-to-all | bytes 2727936 | tf_op jit(solution)/shard_map/all_to_all | solution.py:136
  1467.6 1.5 copy.73
  (578 shorter events, 290.0 us)
Async XLA Ops:
  6.5 161.3 %all-gather.3.cloned.1.call-start = ((), (), s32[]{:S(2)}) async-start(), calls=%async_computation.4 | async-start | bytes 12275712 | tf_op jit(solution)/shard_map/all_gather | solution.py:124
  7.3 299.7 %all-reduce.5.cloned.1.call-start = ((), (), s32[]{:S(2)}) async-start(), calls=%async_computation.6 | async-start | bytes 11534336
  197.5 118.1 %copy-start.82 = (f32[3,144,288]{2,1,0:T(8,128)S(1)}, f32[3,144,288]{2,1,0:T(8,128)}, u32[]{:S(2)}) copy-start(f32[3,144,288]{2,1,0:T(8,128)} %param.13) | copy-start | bytes 1492996
  310.1 39.3 %all-to-all-start = ((bf16[1332,8,1,64]{0,3,2,1:T(8,128)(2,1)}), bf16[1332,8,1,64]{0,3,2,1:T(8,128)(2,1)S(1)}, u32[]{:S(2)}, u32[]{:S(2)}) async-start(bf16[1332,8,1,64]{0,3,2,1:T(8,128)(2,1)} %constant_dynamic-slice_fusion.1), calls=%async_computation | async-start | bytes 2883584 | tf_op jit(solution)/shard_map/all_to_all | solution.py:131
  316.4 232.3 %copy-start.2 = (f32[144,288]{1,0:T(8,128)}, f32[144,288]{1,0:T(8,128)S(1)}, u32[]{:S(2)}) copy-start(f32[144,288]{1,0:T(8,128)S(1)} %get-tuple-element.455) | copy-start | bytes 497668
  316.4 232.3 %copy-start.4 = (f32[144,288]{1,0:T(8,128)}, f32[144,288]{1,0:T(8,128)S(1)}, u32[]{:S(2)}) copy-start(f32[144,288]{1,0:T(8,128)S(1)} %get-tuple-element.456) | copy-start | bytes 497668
  412.4 69.9 %copy-start.8 = (bf16[2,1,64]{1,0,2:T(2,128)(2,1)}, bf16[2,1,64]{1,0,2:T(2,128)(2,1)S(1)}, u32[]{:S(2)}) copy-start(bf16[2,1,64]{1,0,2:T(2,128)(2,1)S(1)} %broadcast.223) | copy-start | bytes 772
  412.4 69.9 %copy-start.10 = (bf16[2,2,64]{1,0,2:T(2,128)(2,1)}, bf16[2,2,64]{1,0,2:T(2,128)(2,1)S(1)}, u32[]{:S(2)}) copy-start(bf16[2,2,64]{1,0,2:T(2,128)(2,1)S(1)} %broadcast.224) | copy-start | bytes 1540
  412.5 69.8 %copy-start.12 = (bf16[2,3,64]{1,0,2:T(2,128)(2,1)}, bf16[2,3,64]{1,0,2:T(2,128)(2,1)S(1)}, u32[]{:S(2)}) copy-start(bf16[2,3,64]{1,0,2:T(2,128)(2,1)S(1)} %broadcast.225) | copy-start | bytes 2308
  412.5 13.8 copy-start.14
  412.6 13.8 copy-start.16
  412.6 13.8 copy-start.18
  412.6 13.7 copy-start.20
  412.7 13.7 copy-start.22
  412.7 13.7 copy-start.24
  412.7 13.7 copy-start.26
  412.8 13.6 copy-start.28
  412.8 13.6 copy-start.30
  548.7 15.2 %copy-start.84 = (f32[144]{0:T(256)S(1)}, f32[144]{0:T(256)}, u32[]{:S(2)}) copy-start(f32[144]{0:T(256)} %constant.9.clone) | copy-start | bytes 1732
  717.9 21.5 %all-to-all-start.1 = ((bf16[4,2664,1,64]{1,3,2,0:T(8,128)(2,1)}), bf16[4,2664,1,64]{1,3,2,0:T(8,128)(2,1)S(1)}, u32[]{:S(2)}, u32[]{:S(2)}) async-start(bf16[4,2664,1,64]{1,3,2,0:T(8,128)(2,1)} %copy.62), calls=%async_computation.1 | async-start | bytes 2752512 | tf_op jit(solution)/shard_map/all_to_all | solution.py:136
  721.4 174.7 %all-gather.5.cloned.1.call-start = ((), (), s32[]{:S(2)}) async-start(), calls=%async_computation.5 | async-start | bytes 12386304 | tf_op jit(solution)/shard_map/all_gather | solution.py:124
  723.3 17.6 %copy-start = (bf16[2664,256]{0,1:T(8,128)(2,1)}, bf16[2664,256]{0,1:T(8,128)(2,1)S(1)}, u32[]{:S(2)}) copy-start(bf16[2664,256]{0,1:T(8,128)(2,1)S(1)} %copy.52) | copy-start | bytes 4091908
  740.9 294.3 %all-reduce.7.cloned.1.call-start = ((), (), s32[]{:S(2)}) async-start(), calls=%async_computation.7 | async-start | bytes 11534336
  1085.8 52.9 %copy-start.9 = (bf16[2,1,64]{1,0,2:T(2,128)(2,1)S(1)}, bf16[2,1,64]{1,0,2:T(2,128)(2,1)}, u32[]{:S(2)}) copy-start(bf16[2,1,64]{1,0,2:T(2,128)(2,1)} %copy-done.8) | copy-start | bytes 772
  1085.8 52.9 %copy-start.11 = (bf16[2,2,64]{1,0,2:T(2,128)(2,1)S(1)}, bf16[2,2,64]{1,0,2:T(2,128)(2,1)}, u32[]{:S(2)}) copy-start(bf16[2,2,64]{1,0,2:T(2,128)(2,1)} %copy-done.10) | copy-start | bytes 1540
  1085.8 52.9 %copy-start.13 = (bf16[2,3,64]{1,0,2:T(2,128)(2,1)S(1)}, bf16[2,3,64]{1,0,2:T(2,128)(2,1)}, u32[]{:S(2)}) copy-start(bf16[2,3,64]{1,0,2:T(2,128)(2,1)} %copy-done.12) | copy-start | bytes 2308
  1085.8 52.9 %copy-start.15 = (bf16[2,4,64]{1,0,2:T(2,128)(2,1)S(1)}, bf16[2,4,64]{1,0,2:T(2,128)(2,1)}, u32[]{:S(2)}) copy-start(bf16[2,4,64]{1,0,2:T(2,128)(2,1)} %copy-done.14) | copy-start | bytes 3076
  1085.8 52.9 %copy-start.17 = (bf16[2,5,64]{1,0,2:T(2,128)(2,1)S(1)}, bf16[2,5,64]{1,0,2:T(2,128)(2,1)}, u32[]{:S(2)}) copy-start(bf16[2,5,64]{1,0,2:T(2,128)(2,1)} %copy-done.16) | copy-start | bytes 3844
  1085.8 52.9 %copy-start.19 = (bf16[2,6,64]{1,0,2:T(2,128)(2,1)S(1)}, bf16[2,6,64]{1,0,2:T(2,128)(2,1)}, u32[]{:S(2)}) copy-start(bf16[2,6,64]{1,0,2:T(2,128)(2,1)} %copy-done.18) | copy-start | bytes 4612
  1085.8 52.9 %copy-start.21 = (bf16[2,7,64]{1,0,2:T(2,128)(2,1)S(1)}, bf16[2,7,64]{1,0,2:T(2,128)(2,1)}, u32[]{:S(2)}) copy-start(bf16[2,7,64]{1,0,2:T(2,128)(2,1)} %copy-done.20) | copy-start | bytes 5380
  1085.8 52.9 %copy-start.23 = (bf16[2,8,64]{1,0,2:T(2,128)(2,1)S(1)}, bf16[2,8,64]{1,0,2:T(2,128)(2,1)}, u32[]{:S(2)}) copy-start(bf16[2,8,64]{1,0,2:T(2,128)(2,1)} %copy-done.22) | copy-start | bytes 6148
  1085.8 52.9 %copy-start.25 = (bf16[2,9,64]{1,0,2:T(2,128)(2,1)S(1)}, bf16[2,9,64]{1,0,2:T(2,128)(2,1)}, u32[]{:S(2)}) copy-start(bf16[2,9,64]{1,0,2:T(2,128)(2,1)} %copy-done.24) | copy-start | bytes 6916
  1085.8 52.9 %copy-start.27 = (bf16[2,10,64]{1,0,2:T(2,128)(2,1)S(1)}, bf16[2,10,64]{1,0,2:T(2,128)(2,1)}, u32[]{:S(2)}) copy-start(bf16[2,10,64]{1,0,2:T(2,128)(2,1)} %copy-done.26) | copy-start | bytes 7684
  1085.8 52.9 %copy-start.29 = (bf16[2,11,64]{1,0,2:T(2,128)(2,1)S(1)}, bf16[2,11,64]{1,0,2:T(2,128)(2,1)}, u32[]{:S(2)}) copy-start(bf16[2,11,64]{1,0,2:T(2,128)(2,1)} %copy-done.28) | copy-start | bytes 8452
  1085.9 52.9 %copy-start.31 = (bf16[2,12,64]{1,0,2:T(2,128)(2,1)S(1)}, bf16[2,12,64]{1,0,2:T(2,128)(2,1)}, u32[]{:S(2)}) copy-start(bf16[2,12,64]{1,0,2:T(2,128)(2,1)} %copy-done.30) | copy-start | bytes 9220
  1085.9 52.9 %copy-start.33 = (bf16[2,13,64]{1,0,2:T(2,128)(2,1)S(1)}, bf16[2,13,64]{1,0,2:T(2,128)(2,1)}, u32[]{:S(2)}) copy-start(bf16[2,13,64]{1,0,2:T(2,128)(2,1)} %copy-done.32) | copy-start | bytes 9988
  1085.9 52.9 %copy-start.35 = (bf16[2,14,64]{1,0,2:T(2,128)(2,1)S(1)}, bf16[2,14,64]{1,0,2:T(2,128)(2,1)}, u32[]{:S(2)}) copy-start(bf16[2,14,64]{1,0,2:T(2,128)(2,1)} %copy-done.34) | copy-start | bytes 10756
  1085.9 52.9 %copy-start.37 = (bf16[2,15,64]{1,0,2:T(2,128)(2,1)S(1)}, bf16[2,15,64]{1,0,2:T(2,128)(2,1)}, u32[]{:S(2)}) copy-start(bf16[2,15,64]{1,0,2:T(2,128)(2,1)} %copy-done.36) | copy-start | bytes 11524
  1085.9 52.9 %copy-start.39 = (bf16[2,16,64]{1,0,2:T(2,128)(2,1)S(1)}, bf16[2,16,64]{1,0,2:T(2,128)(2,1)}, u32[]{:S(2)}) copy-start(bf16[2,16,64]{1,0,2:T(2,128)(2,1)} %copy-done.38) | copy-start | bytes 12292
  1085.9 52.9 %copy-start.41 = (bf16[2,17,64]{1,0,2:T(2,128)(2,1)S(1)}, bf16[2,17,64]{1,0,2:T(2,128)(2,1)}, u32[]{:S(2)}) copy-start(bf16[2,17,64]{1,0,2:T(2,128)(2,1)} %copy-done.40) | copy-start | bytes 13060
  1085.9 52.9 %copy-start.43 = (bf16[2,18,64]{1,0,2:T(2,128)(2,1)S(1)}, bf16[2,18,64]{1,0,2:T(2,128)(2,1)}, u32[]{:S(2)}) copy-start(bf16[2,18,64]{1,0,2:T(2,128)(2,1)} %copy-done.42) | copy-start | bytes 13828
  1085.9 52.9 %copy-start.45 = (bf16[2,19,64]{1,0,2:T(2,128)(2,1)S(1)}, bf16[2,19,64]{1,0,2:T(2,128)(2,1)}, u32[]{:S(2)}) copy-start(bf16[2,19,64]{1,0,2:T(2,128)(2,1)} %copy-done.44) | copy-start | bytes 14596
  1085.9 52.9 %copy-start.47 = (bf16[2,20,64]{1,0,2:T(2,128)(2,1)S(1)}, bf16[2,20,64]{1,0,2:T(2,128)(2,1)}, u32[]{:S(2)}) copy-start(bf16[2,20,64]{1,0,2:T(2,128)(2,1)} %copy-done.46) | copy-start | bytes 15364
  1086.0 52.9 %copy-start.49 = (bf16[2,21,64]{1,0,2:T(2,128)(2,1)S(1)}, bf16[2,21,64]{1,0,2:T(2,128)(2,1)}, u32[]{:S(2)}) copy-start(bf16[2,21,64]{1,0,2:T(2,128)(2,1)} %copy-done.48) | copy-start | bytes 16132
  1086.0 52.9 %copy-start.51 = (bf16[2,22,64]{1,0,2:T(2,128)(2,1)S(1)}, bf16[2,22,64]{1,0,2:T(2,128)(2,1)}, u32[]{:S(2)}) copy-start(bf16[2,22,64]{1,0,2:T(2,128)(2,1)} %copy-done.50) | copy-start | bytes 16900
  1086.0 52.9 %copy-start.53 = (bf16[2,23,64]{1,0,2:T(2,128)(2,1)S(1)}, bf16[2,23,64]{1,0,2:T(2,128)(2,1)}, u32[]{:S(2)}) copy-start(bf16[2,23,64]{1,0,2:T(2,128)(2,1)} %copy-done.52) | copy-start | bytes 17668
  1086.0 52.9 %copy-start.55 = (bf16[2,24,64]{1,0,2:T(2,128)(2,1)S(1)}, bf16[2,24,64]{1,0,2:T(2,128)(2,1)}, u32[]{:S(2)}) copy-start(bf16[2,24,64]{1,0,2:T(2,128)(2,1)} %copy-done.54) | copy-start | bytes 18436
  1086.0 52.9 %copy-start.57 = (bf16[2,25,64]{1,0,2:T(2,128)(2,1)S(1)}, bf16[2,25,64]{1,0,2:T(2,128)(2,1)}, u32[]{:S(2)}) copy-start(bf16[2,25,64]{1,0,2:T(2,128)(2,1)} %copy-done.56) | copy-start | bytes 19204
  1086.0 52.9 %copy-start.59 = (bf16[2,26,64]{1,0,2:T(2,128)(2,1)S(1)}, bf16[2,26,64]{1,0,2:T(2,128)(2,1)}, u32[]{:S(2)}) copy-start(bf16[2,26,64]{1,0,2:T(2,128)(2,1)} %copy-done.58) | copy-start | bytes 19972
  1086.0 52.9 %copy-start.61 = (bf16[2,27,64]{1,0,2:T(2,128)(2,1)S(1)}, bf16[2,27,64]{1,0,2:T(2,128)(2,1)}, u32[]{:S(2)}) copy-start(bf16[2,27,64]{1,0,2:T(2,128)(2,1)} %copy-done.60) | copy-start | bytes 20740
  1086.0 52.9 %copy-start.63 = (bf16[2,28,64]{1,0,2:T(2,128)(2,1)S(1)}, bf16[2,28,64]{1,0,2:T(2,128)(2,1)}, u32[]{:S(2)}) copy-start(bf16[2,28,64]{1,0,2:T(2,128)(2,1)} %copy-done.62) | copy-start | bytes 21508
  1086.0 52.9 %copy-start.65 = (bf16[2,29,64]{1,0,2:T(2,128)(2,1)S(1)}, bf16[2,29,64]{1,0,2:T(2,128)(2,1)}, u32[]{:S(2)}) copy-start(bf16[2,29,64]{1,0,2:T(2,128)(2,1)} %copy-done.64) | copy-start | bytes 22276
  1086.0 52.9 %copy-start.67 = (bf16[2,30,64]{1,0,2:T(2,128)(2,1)S(1)}, bf16[2,30,64]{1,0,2:T(2,128)(2,1)}, u32[]{:S(2)}) copy-start(bf16[2,30,64]{1,0,2:T(2,128)(2,1)} %copy-done.66) | copy-start | bytes 23044
  1086.0 52.9 %copy-start.69 = (bf16[2,31,64]{1,0,2:T(2,128)(2,1)S(1)}, bf16[2,31,64]{1,0,2:T(2,128)(2,1)}, u32[]{:S(2)}) copy-start(bf16[2,31,64]{1,0,2:T(2,128)(2,1)} %copy-done.68) | copy-start | bytes 23812
  1086.1 52.9 %copy-start.71 = (bf16[2,32,64]{1,0,2:T(2,128)(2,1)S(1)}, bf16[2,32,64]{1,0,2:T(2,128)(2,1)}, u32[]{:S(2)}) copy-start(bf16[2,32,64]{1,0,2:T(2,128)(2,1)} %copy-done.70) | copy-start | bytes 24580
  1086.1 52.9 %copy-start.73 = (bf16[2,33,64]{1,0,2:T(2,128)(2,1)S(1)}, bf16[2,33,64]{1,0,2:T(2,128)(2,1)}, u32[]{:S(2)}) copy-start(bf16[2,33,64]{1,0,2:T(2,128)(2,1)} %copy-done.72) | copy-start | bytes 25348
  1086.1 52.9 %copy-start.75 = (bf16[2,34,64]{1,0,2:T(2,128)(2,1)S(1)}, bf16[2,34,64]{1,0,2:T(2,128)(2,1)}, u32[]{:S(2)}) copy-start(bf16[2,34,64]{1,0,2:T(2,128)(2,1)} %copy-done.74) | copy-start | bytes 26116
  1086.1 52.9 %copy-start.77 = (bf16[2,35,64]{1,0,2:T(2,128)(2,1)S(1)}, bf16[2,35,64]{1,0,2:T(2,128)(2,1)}, u32[]{:S(2)}) copy-start(bf16[2,35,64]{1,0,2:T(2,128)(2,1)} %copy-done.76) | copy-start | bytes 26884
  1086.1 52.9 %copy-start.79 = (bf16[2,36,64]{1,0,2:T(2,128)(2,1)S(1)}, bf16[2,36,64]{1,0,2:T(2,128)(2,1)}, u32[]{:S(2)}) copy-start(bf16[2,36,64]{1,0,2:T(2,128)(2,1)} %copy-done.78) | copy-start | bytes 27652
  1086.1 52.9 %copy-start.81 = (bf16[2,37,64]{1,0,2:T(2,128)(2,1)S(1)}, bf16[2,37,64]{1,0,2:T(2,128)(2,1)}, u32[]{:S(2)}) copy-start(bf16[2,37,64]{1,0,2:T(2,128)(2,1)} %copy-done.80) | copy-start | bytes 28420
  1225.0 39.5 %copy-start.3 = (f32[144,288]{1,0:T(8,128)S(1)}, f32[144,288]{1,0:T(8,128)}, u32[]{:S(2)}) copy-start(f32[144,288]{1,0:T(8,128)} %copy-done.2) | copy-start | bytes 497668
  1225.0 39.5 %copy-start.5 = (f32[144,288]{1,0:T(8,128)S(1)}, f32[144,288]{1,0:T(8,128)}, u32[]{:S(2)}) copy-start(f32[144,288]{1,0:T(8,128)} %copy-done.4) | copy-start | bytes 497668
  1264.6 15.2 %copy-start.85 = (f32[144]{0:T(256)S(1)}, f32[144]{0:T(256)}, u32[]{:S(2)}) copy-start(f32[144]{0:T(256)} %constant.9.clone) | copy-start | bytes 1732
  1446.5 20.8 %copy-start.1 = (bf16[2664,256]{0,1:T(8,128)(2,1)S(1)}, bf16[2664,256]{0,1:T(8,128)(2,1)}, u32[]{:S(2)}) copy-start(bf16[2664,256]{0,1:T(8,128)(2,1)} %copy-done) | copy-start | bytes 4091908
  (28 other events, 358.0 us)
Sparse Core Ops, SparseCore 0:
  9.4 158.4 all-gather.2
  197.6 109.2 all-reduce.4
  741.0 155.0 all-gather.4
  925.9 109.2 all-reduce.6
where the time goes:
time: 1500 us; the launch traced here: 1480 us
  waiting for transfers between devices  583 us (39%)
  local copies, waits for them, and re-layouts  548 us (37%)
  matrix products  219 us (15%)
  blocking collectives  60 us (4%)
  other arithmetic  40.8 us (3%)
  between operations  16.1 us (1%)
    all_gather x2, waiting for transfers between devices, body(): lax.all_gather(current, 'row', axis=1, tiled=True)  316 us
    unnamed x6, waiting for transfers between devices  218 us
    squeeze x161, local copies, waits for them, and re-layouts, pick_levels(): pieces.append(projected[:, freq_index, skip:, :])  188 us
    unnamed x180, local copies, waits for them, and re-layouts  134 us
    slice x174, local copies, waits for them, and re-layouts, spread_levels(): pieces.append(halves[:, start:start + count, :])  99.9 us
    dot_general x2, matrix products, contrast_apply(): jnp.einsum('cktq,qp->cktp', latitude, fourier, precision=triple, preferre...  79.2 us
    dot_general x2, local copies, waits for them, and re-layouts, contrast_apply(): jnp.einsum('cktp,qp->cktq', weighted, fourier, precision=triple, preferre...  44.3 us
    dot_general x2, matrix products, body(): jnp.dot(tmatrix, lax.all_gather(current, 'row', axis=1, tiled=True), pref...  42.9 us
  transfers between devices with their start and end apart: 6, of which 6 were waited for; matrix products, arithmetic and copies ran while one was open for 0% of the time, Pallas kernels for 0%

commit v1 on v0

v1 whole, which is shorter than its diff:
```python
import functools
import jax
import jax.numpy as jnp
import numpy as np
from jax import lax
from jax.experimental import pallas as pl
from jax.experimental.pallas import tpu as pltpu
from jax.sharding import PartitionSpec as P

ITERS = 2

def angular_tables(degree):
    lat_count = 2 * degree
    lon_count = 4 * degree
    colatitude = (np.arange(lat_count) + 0.5) * np.pi / lat_count
    cos_col = np.cos(colatitude)
    sin_col = np.sin(colatitude)
    legendre = np.zeros((degree + 1, degree, lat_count))
    diagonal_term = np.full(lat_count, np.sqrt(0.5))
    for order_m in range(degree + 1):
        if order_m > 0:
            diagonal_term = (
                diagonal_term * np.sqrt((2.0 * order_m + 1.0) / (2.0 * order_m)) * sin_col
            )
        earlier = np.zeros(lat_count)
        latest = diagonal_term
        for degree_l in range(order_m, degree + 1):
            if degree_l == order_m:
                current = diagonal_term
            elif degree_l == order_m + 1:
                current = np.sqrt(2.0 * order_m + 3.0) * cos_col * diagonal_term
            else:
                factor_a = np.sqrt((4.0 * degree_l**2 - 1.0) / (degree_l**2 - order_m**2))
                factor_b = np.sqrt(
                    ((degree_l - 1.0) ** 2 - order_m**2) / (4.0 * (degree_l - 1.0) ** 2 - 1.0)
                )
                current = factor_a * (cos_col * latest - factor_b * earlier)
            if degree_l > order_m:
                earlier, latest = (latest, current)
            if degree_l >= 1:
                legendre[order_m, degree_l - 1] = current
    angle = 2.0 * np.pi * np.arange(lon_count) / lon_count
    cosines = np.cos(np.arange(degree + 1)[:, None] * angle) / np.sqrt(np.pi)
    cosines[0] = 1.0 / np.sqrt(2.0 * np.pi)
    sines = np.sin(np.arange(degree + 1)[:, None] * angle) / np.sqrt(np.pi)
    weight = sin_col * (np.pi / lat_count) * (2.0 * np.pi / lon_count)
    return legendre, cosines, sines, weight


def up(value, unit):
    return -(-value // unit) * unit


def split(table):
    high = table.astype(np.float32).astype(jnp.bfloat16)
    low = (table - high.astype(np.float64)).astype(jnp.bfloat16)
    return high, low


@functools.lru_cache(maxsize=None)
def shell_tables(degree):
    legendre, cosines, sines, weight = angular_tables(degree)
    lat_count, half = 2 * degree, 2 * degree
    slots = up(degree + 1, 16)
    window = up(degree + 7, 16)
    pairs = up(half + 1, 8)
    starts = np.cumsum([0, degree] + [degree + 1 - m for m in range(1, degree + 1)])
    cosine_rows = int(starts[-1])
    sine_shift = -(cosine_rows - degree) % 8
    offsets = np.zeros(slots, np.int32)
    shifted = np.zeros((slots, window, lat_count))
    for m in range(degree + 1):
        offsets[m] = starts[m] // 8 * 8
        first = max(m - 1, 0)
        place = starts[m] - offsets[m]
        shifted[m, place : place + degree - first] = legendre[m, first:]
    high, low = split(shifted)
    synth = np.concatenate([high, low], axis=1).transpose(0, 2, 1)
    analyse = np.concatenate([high, low], axis=1)
    fold = np.zeros((2, slots, pairs))
    fold[0, : degree + 1, : half + 1] = cosines[:, : half + 1]
    fold[1, : degree + 1, 1:half] = sines[:, 1:half]
    fhigh, flow = split(fold)
    inverse = np.concatenate([fhigh, flow], axis=1).transpose(0, 2, 1)
    forward = np.concatenate([fhigh, flow], axis=1)
    return dict(
        slots=slots, window=window, pairs=pairs, cosine_rows=cosine_rows,
        sine_shift=sine_shift, sine_gap=cosine_rows - degree + sine_shift,
        offsets=offsets, synth=np.ascontiguousarray(synth), analyse=analyse,
        inverse=np.ascontiguousarray(inverse), forward=forward, weight=weight,
    )


GROUP = 32


def arrange_contrast(contrast, table):
    comps, lat_count, lon_count = contrast.shape
    half, pairs = lon_count // 2, table["pairs"]
    scaled = contrast * jnp.asarray(table["weight"], jnp.float32)[:, None]
    plus = jnp.pad(scaled[:, :, : half + 1], ((0, 0), (0, 0), (0, pairs - half - 1)))
    minus = jnp.pad(scaled[:, :, half + 1 :][:, :, ::-1], ((0, 0), (0, 0), (1, pairs - half)))
    both = jnp.stack([plus, minus])
    groups = -(-lat_count // GROUP)
    both = jnp.pad(both, ((0, 0), (0, 1), (0, groups * GROUP - lat_count), (0, 0)))
    both = both.reshape(2, comps + 1, groups, GROUP, pairs)
    return both.transpose(2, 0, 4, 3, 1).reshape(groups, 2, pairs, GROUP * (comps + 1))


def shell_kernel(table, unroll, scalar_ref, x_ref, con_ref, synth_ref, analyse_ref, inverse_ref,
                 forward_ref, o_ref, rows_ref, grid_ref):
    slots, window, pairs = table["slots"], table["window"], table["pairs"]
    cosine_rows, gap, shift = table["cosine_rows"], table["sine_gap"], table["sine_shift"]
    lat_count = synth_ref.shape[1]
    pieces, columns, length = x_ref.shape
    full = pieces * length // 2
    lanes = 2 * columns
    f32, bf16 = jnp.float32, jnp.bfloat16

    def place(row):
        return row if row < cosine_rows else row + shift

    cut = cosine_rows // 8 * 8
    rows_ref[cut : cut + 16, :] = jnp.zeros((16, lanes), f32)
    tail = (full + shift) // 8 * 8
    rows_ref[tail:, :] = jnp.zeros((rows_ref.shape[0] - tail, lanes), f32)
    for piece in range(pieces // 2):
        upper = scalar_ref[slots + piece]
        lower = scalar_ref[slots + piece + pieces // 2]
        for start in range(0, length, 128):
            size = min(128, length - start)
            block = jnp.concatenate(
                [x_ref[upper, :, start : start + size], x_ref[lower, :, start : start + size]], axis=0
            ).astype(f32)
            turned = block.T
            base = piece * length + start
            if base < cosine_rows < base + size:
                first = cosine_rows - base
                rows_ref[base : base + first, :] = turned[:first]
                rows_ref[base + first + shift : base + size + shift, :] = turned[first:]
            else:
                rows_ref[place(base) : place(base) + size, :] = turned

    def synthesis(step, carry):
        for inner in range(unroll[0]):
            m = step * unroll[0] + inner
            off = pl.multiple_of(scalar_ref[m], 8)
            both = jnp.concatenate(
                [rows_ref[pl.ds(off, window), :], rows_ref[pl.ds(off + gap, window), :]], axis=1
            ).astype(bf16)
            out = jnp.dot(synth_ref[m], jnp.concatenate([both, both], axis=0), preferred_element_type=f32)
            grid_ref[pl.ds(m, lat_count, stride=2 * slots), :] = out[:, :lanes]
            grid_ref[pl.ds(m + slots, lat_count, stride=2 * slots), :] = out[:, lanes:]
        return carry

    lax.fori_loop(0, slots // unroll[0], synthesis, 0)

    lane = lax.broadcasted_iota(jnp.int32, (pairs, lanes), 1)
    own = jnp.where(lane < columns, 0, 2)

    def longitude(step, carry):
        for inner in range(unroll[1]):
            pair = step * unroll[1] + inner
            base = [pl.multiple_of((2 * pair + j) * 2 * slots, 8) for j in range(2)]
            cos_in = jnp.concatenate([grid_ref[pl.ds(b, slots), :] for b in base], axis=1).astype(bf16)
            sin_in = jnp.concatenate([grid_ref[pl.ds(b + slots, slots), :] for b in base], axis=1).astype(bf16)
            even = jnp.dot(inverse_ref[0], jnp.concatenate([cos_in, cos_in], axis=0), preferred_element_type=f32)
            odd = jnp.dot(inverse_ref[1], jnp.concatenate([sin_in, sin_in], axis=0), preferred_element_type=f32)
            evens, odds = [], []
            for j in range(2):
                t = 2 * pair + j
                part = slice(j * lanes, (j + 1) * lanes)
                lane_base = (t % GROUP) * 4
                vals = []
                for sign in range(2):
                    surface = even[:, part] + odd[:, part] if sign == 0 else even[:, part] - odd[:, part]
                    source = con_ref[t // GROUP, sign]
                    own_c = jnp.take_along_axis(source, own + lane_base, axis=1)
                    cross_c = jnp.take_along_axis(source, jnp.full((pairs, lanes), 1, jnp.int32) + lane_base, axis=1)
                    vals.append(own_c * surface + cross_c * pltpu.roll(surface, columns, 1))
                evens.append(vals[0] + vals[1])
                odds.append(vals[0] - vals[1])
            evens = jnp.concatenate(evens, axis=1).astype(bf16)
            odds = jnp.concatenate(odds, axis=1).astype(bf16)
            back = jnp.dot(forward_ref[0], evens, preferred_element_type=f32)
            back = back[:slots] + back[slots:]
            for j in range(2):
                grid_ref[pl.ds(base[j], slots), :] = back[:, j * lanes : (j + 1) * lanes]
            back = jnp.dot(forward_ref[1], odds, preferred_element_type=f32)
            back = back[:slots] + back[slots:]
            for j in range(2):
                grid_ref[pl.ds(base[j] + slots, slots), :] = back[:, j * lanes : (j + 1) * lanes]
        return carry

    lax.fori_loop(0, lat_count // 2 // unroll[1], longitude, 0)

    rows_ref[...] = jnp.zeros(rows_ref.shape, f32)

    def analysis(step, carry):
        for inner in range(unroll[2]):
            m = step * unroll[2] + inner
            off = pl.multiple_of(scalar_ref[m], 8)
            both = jnp.concatenate(
                [grid_ref[pl.ds(m, lat_count, stride=2 * slots), :],
                 grid_ref[pl.ds(m + slots, lat_count, stride=2 * slots), :]], axis=1
            ).astype(bf16)
            out = jnp.dot(analyse_ref[m], both, preferred_element_type=f32)
            out = out[:window] + out[window:]
            rows_ref[pl.ds(off, window), :] += out[:, :lanes]
            rows_ref[pl.ds(off + gap, window), :] += out[:, lanes:]
        return carry

    lax.fori_loop(0, slots // unroll[2], analysis, 0)

    blocks = o_ref.shape[0]
    mine = scalar_ref[slots + pieces]
    size_out = o_ref.shape[2]
    for block in range(blocks // 2):
        for start in range(0, size_out, 128):
            size = min(128, size_out - start)
            base = block * size_out + start
            if base < cosine_rows < base + size:
                value = jnp.concatenate(
                    [rows_ref[base:cosine_rows, :], rows_ref[cosine_rows + shift : base + size + shift, :]], axis=0
                )
            else:
                value = rows_ref[place(base) : place(base) + size, :]
            turned = value.T.astype(bf16)
            o_ref[block ^ mine, :, start : start + size] = turned[:columns]
            o_ref[(block + blocks // 2) ^ mine, :, start : start + size] = turned[columns:]


def couple(scalars, arrived, arranged, table, blocks, unroll=(4, 1, 4)):
    pieces, columns, length = arrived.shape
    full = pieces * length // 2
    lat_count = table["synth"].shape[1]
    rows = up(int(table["offsets"].max()) + table["sine_gap"] + table["window"], 8)
    vm = pl.BlockSpec(memory_space=pltpu.VMEM)
    return pl.pallas_call(
        functools.partial(shell_kernel, table, unroll),
        out_shape=jax.ShapeDtypeStruct((blocks, columns, pieces * length // blocks), jnp.bfloat16),
        in_specs=[pl.BlockSpec(memory_space=pltpu.SMEM)] + [vm] * 6,
        out_specs=vm,
        scratch_shapes=[
            pltpu.VMEM((rows, 2 * columns), jnp.float32),
            pltpu.VMEM((lat_count * 2 * table["slots"], 2 * columns), jnp.float32),
        ],
        cost_estimate=pl.CostEstimate(
            flops=16 * full * lat_count * 2 * columns, bytes_accessed=16 << 20, transcendentals=0
        ),
        compiler_params=pltpu.CompilerParams(vmem_limit_bytes=60 << 20),
    )(scalars, arrived, arranged, jnp.asarray(table["synth"]), jnp.asarray(table["analyse"]),
      jnp.asarray(table["inverse"]), jnp.asarray(table["forward"]))


def ring_of(mesh):
    count = mesh.devices.shape[0]
    spots = [getattr(d, "coords", None) for d in mesh.devices[:, 0]]
    plain = list(range(count))
    if any(s is None for s in spots):
        return plain
    moving = [a for a in range(len(spots[0])) if len({s[a] for s in spots}) > 1]
    if len(moving) != 2:
        return plain
    sizes = {a: len({s[a] for s in spots}) for a in moving}
    even = sorted((a for a in moving if sizes[a] % 2 == 0), key=lambda a: sizes[a])
    if not even or sizes[moving[0]] * sizes[moving[1]] != count:
        return plain
    outer = even[0]
    inner = moving[0] if moving[1] == outer else moving[1]
    where = {(s[outer], s[inner]): i for i, s in enumerate(spots)}
    first = sorted({s[outer] for s in spots})
    second = sorted({s[inner] for s in spots})
    path = []
    for step, i in enumerate(first):
        path += [(i, j) for j in (second[1:] if step % 2 == 0 else second[:0:-1])]
    path += [(i, second[0]) for i in reversed(first)]
    return [where[p] for p in path]


def body(order, tmatrix, panel, contrast):
    row_count, col_count = lax.axis_size("row"), lax.axis_size("col")
    mine_row, mine_col = lax.axis_index("row"), lax.axis_index("col")
    depth, width = panel.shape
    per_device = width // col_count
    local_rows = tmatrix.shape[0]
    table = shell_tables(contrast.shape[1] // 2)
    arranged = arrange_contrast(contrast, table)
    position = np.argsort(np.array(order))
    distance = (jnp.asarray(position, jnp.int32) - jnp.asarray(position, jnp.int32)[mine_row]) % row_count
    scalars = jnp.concatenate([jnp.asarray(table["offsets"]), distance, mine_col[None].astype(jnp.int32)])

    def around(value, hops):
        pairs = [(order[i], order[(i + hops) % row_count]) for i in range(row_count)]
        return lax.ppermute(value, "row", pairs)

    def across(value, flip):
        return lax.ppermute(value, "col", [(i, i ^ flip) for i in range(col_count)])

    def scatter(block):
        product = lax.dot_general(
            block.reshape(-1, depth), tmatrix, (((1,), (1,)), ((), ())), preferred_element_type=jnp.float32
        ).astype(jnp.bfloat16)
        product = product.reshape(block.shape[:-1] + (local_rows,))
        total = product[:, 0].astype(jnp.float32)
        for flip in range(1, col_count):
            total = total + across(product[:, flip], flip).astype(jnp.float32)
        return total.astype(jnp.bfloat16)

    turned = panel.T.reshape(col_count, per_device, depth)
    start = jnp.stack([lax.dynamic_index_in_dim(turned, mine_col ^ j, 0, keepdims=False) for j in range(col_count)])
    current = start
    for iteration in range(ITERS):
        held = [None] * row_count
        held[0] = scatter(current[None])[0]
        ahead = behind = current
        for hop in range(1, (row_count - 1) // 2 + 1):
            ahead, behind = around(ahead, 1), around(behind, -1)
            sums = scatter(jnp.stack([ahead, behind]))
            held[row_count - hop] = around(sums[1], hop)
            held[hop] = around(sums[0], -hop)
        if row_count % 2 == 0:
            cut = per_device // 2
            ahead, behind = around(ahead[:, :cut], 1), around(behind[:, cut:], -1)
            sums = scatter(jnp.concatenate([ahead, behind], axis=1)[None])[0]
            held[row_count // 2] = around(sums, row_count // 2)
        coupled = couple(scalars, jnp.stack(held), arranged, table, col_count)
        pieces = [coupled[0]] + [across(coupled[j], j) for j in range(1, col_count)]
        current = (start.astype(jnp.float32) + jnp.stack(pieces).astype(jnp.float32)).astype(jnp.bfloat16)
    result = jnp.stack([lax.dynamic_index_in_dim(current, mine_col ^ j, 0, keepdims=False) for j in range(col_count)])
    return result.reshape(width, depth).T


def solution(mesh):
    placed = (P("row", "col"), P("col", "row"), P())
    return jax.shard_map(
        functools.partial(body, ring_of(mesh)),
        mesh=mesh, in_specs=placed, out_specs=P("col", "row"), check_vma=False,
    )
```

time: 1500 us -> 609 us (0.41)
  local copies, waits for them, and re-layouts: 548 us -> 57.6 us
  waiting for transfers between devices: 583 us -> 230 us
  matrix products: 219 us -> 68.6 us
  Pallas kernels: 0 us -> 146 us
  starting transfers between devices: 9.18 us -> 78 us
  blocking collectives: 60 us -> 0 us
  other arithmetic: 40.8 us -> 15.7 us
    all_gather x2 -> x0, waiting for transfers between devices: 316 us -> none  [body(): lax.all_gather(current, 'row', axis=1, tiled=True)]
    ppermute x0 -> x66, waiting for transfers between devices: none -> 230 us  [the longest x30 122 us: around(): return lax.ppermute(value, 'row', pairs)]
    unnamed x6 -> x0, waiting for transfers between devices: 218 us -> none
    squeeze x161 -> x16, local copies, waits for them, and re-layouts: 188 us -> 5.41 us  [the longest x6 3.15 us: body(): held[row_count - hop] = around(sums[1], hop)]
    dot_general x10, matrix products: 219 us -> 68.6 us  [scatter(): lax.dot_general(block.reshape(-1, depth), tmatrix, (((1,), (1,)), ((), ()...]
    pallas_call x0 -> x2, Pallas kernels: none -> 146 us  [couple(): pl.pallas_call(functools.partial(shell_kernel, table, unroll), out_shape=...]
    unnamed x180 -> x72, local copies, waits for them, and re-layouts: 134 us -> 24.3 us
    slice x174 -> x7, local copies, waits for them, and re-layouts: 99.9 us -> 3.98 us  [the longest x2 2.84 us: body(): pieces = [coupled[0]] + [across(coupled[j], j) for j in range(1, col_count)]]
  transfers between devices with their start and end apart: 6 -> 66, of which waited for: 6 -> 37; matrix products, arithmetic and copies ran while one was open for 0% -> 21% of each run, Pallas kernels for 0% -> 0%
where the time goes in v1:
time: 609 us; the launch traced here: 597 us
  waiting for transfers between devices  230 us (38%)
  Pallas kernels  146 us (24%)
  starting transfers between devices  78 us (13%)
  matrix products  68.6 us (11%)
  local copies, waits for them, and re-layouts  57.6 us (9%)
  other arithmetic  15.7 us (3%)
    pallas_call x2, Pallas kernels, couple(): pl.pallas_call(functools.partial(shell_kernel, table, unroll), out_shape=...  146 us
    ppermute x30, waiting for transfers between devices, around(): return lax.ppermute(value, 'row', pairs)  122 us
    ppermute x36, waiting for transfers between devices, across(): return lax.ppermute(value, 'col', [(i, i ^ flip) for i in range(col_count)])  108 us
    dot_general x10, matrix products, scatter(): lax.dot_general(block.reshape(-1, depth), tmatrix, (((1,), (1,)), ((), ()...  68.6 us
    ppermute x30, starting transfers between devices, around(): return lax.ppermute(value, 'row', pairs)  55 us
    unnamed x72, local copies, waits for them, and re-layouts  24.3 us
    ppermute x36, starting transfers between devices, across(): return lax.ppermute(value, 'col', [(i, i ^ flip) for i in range(col_count)])  23 us
    convert_element_type x10, local copies, waits for them, and re-layouts, scatter(): product = lax.dot_general(block.reshape(-1, depth), tmatrix, (((1,), (1,)...  13.4 us
  transfers between devices with their start and end apart: 66, of which 37 were waited for; matrix products, arithmetic and copies ran while one was open for 21% of the time, Pallas kernels for 0%

profile of v1, /device:TPU:0, one launch (start us, length us, event | category | flops | bytes accessed | tf_op | source)
XLA Modules:
  0.0 597.4 jit_solution(18305602319960127518)
XLA Ops:
  2.7 3.0 collective-permute-start.4
  5.8 5.2 convolution_convert_fusion.9
  15.3 5.3 reverse
  22.2 2.1 copy.38.con_ref
  26.2 9.8 %collective-permute-done.4 = bf16[4,64,2664]{2,1,0:T(8,128)(2,1)} collective-permute-done((bf16[4,64,2664]{2,1,0:T(8,128)(2,1)S(1)}, bf16[4,64,2664]{2,1,0:T(8,128)(2,1)}, u32[]{:S(2)}, u32[]{:S(2)}) %collective-permute-start.4) | collective-permute-done | bytes 1364000 | tf_op jit(solution)/shard_map/ppermute | solution.py:295
  37.4 2.0 pad_maximum_fusion
  39.4 8.4 %convolution_convert_fusion.5 = bf16[512,1332]{0,1:T(8,128)(2,1)} fusion(bf16[512,2664]{1,0:T(8,128)(2,1)S(1)} %bitcast.332, bf16[1332,2664]{1,0:T(8,128)(2,1)} %param.11), kind=kOutput, calls=%fused_computation.7 | convolution fusion | flops 3634292736 | bytes 11188800 | tf_op jit(solution)/shard_map/dot_general | solution.py:301
  47.8 1.8 copy.21
  53.7 2.0 fusion.34
  55.6 4.8 collective-permute-done.7
  60.4 7.8 %collective-permute-done.6 = bf16[2,64,1332]{2,1,0:T(8,128)(2,1)S(1)} collective-permute-done((bf16[2,64,1332]{2,1,0:T(8,128)(2,1)S(1)}, bf16[2,64,1332]{2,1,0:T(8,128)(2,1)S(1)}, u32[]{:S(2)}, u32[]{:S(2)}) %collective-permute-start.6) | collective-permute-done | bytes 341024 | tf_op jit(solution)/shard_map/ppermute | solution.py:298
  70.7 14.2 %collective-permute-done.10 = bf16[4,64,2664]{2,1,0:T(8,128)(2,1)S(1)} collective-permute-done((bf16[4,64,2664]{2,1,0:T(8,128)(2,1)}, bf16[4,64,2664]{2,1,0:T(8,128)(2,1)S(1)}, u32[]{:S(2)}, u32[]{:S(2)}) %collective-permute-start.10) | collective-permute-done | bytes 1364000 | tf_op jit(solution)/shard_map/ppermute | solution.py:295
  86.6 8.3 %convolution_convert_fusion.4 = bf16[512,1332]{0,1:T(8,128)(2,1)} fusion(bf16[512,2664]{1,0:T(8,128)(2,1)S(1)} %bitcast.333, bf16[1332,2664]{1,0:T(8,128)(2,1)} %param.11), kind=kOutput, calls=%fused_computation.6 | convolution fusion | flops 3634292736 | bytes 11188800 | tf_op jit(solution)/shard_map/dot_general | solution.py:301
  94.9 1.8 copy.26
  102.5 5.0 collective-permute-done.13
  107.6 7.6 %collective-permute-done.12 = bf16[2,64,1332]{2,1,0:T(8,128)(2,1)S(1)} collective-permute-done((bf16[2,64,1332]{2,1,0:T(8,128)(2,1)S(1)}, bf16[2,64,1332]{2,1,0:T(8,128)(2,1)S(1)}, u32[]{:S(2)}, u32[]{:S(2)}) %collective-permute-start.12) | collective-permute-done | bytes 341024 | tf_op jit(solution)/shard_map/ppermute | solution.py:298
  116.2 2.6 collective-permute-start.14
  118.8 14.1 %collective-permute-done.16 = bf16[4,64,2664]{2,1,0:T(8,128)(2,1)S(1)} collective-permute-done((bf16[4,64,2664]{2,1,0:T(8,128)(2,1)S(1)}, bf16[4,64,2664]{2,1,0:T(8,128)(2,1)S(1)}, u32[]{:S(2)}, u32[]{:S(2)}) %collective-permute-start.16) | collective-permute-done | bytes 1364000 | tf_op jit(solution)/shard_map/ppermute | solution.py:295
  134.4 8.3 %convolution_convert_fusion.3 = bf16[512,1332]{0,1:T(8,128)(2,1)} fusion(bf16[512,2664]{1,0:T(8,128)(2,1)S(1)} %bitcast.334, bf16[1332,2664]{1,0:T(8,128)(2,1)} %param.11), kind=kOutput, calls=%fused_computation.5 | convolution fusion | flops 3634292736 | bytes 11188800 | tf_op jit(solution)/shard_map/dot_general | solution.py:301
  142.8 1.8 copy.31
  150.5 5.0 collective-permute-done.19
  156.3 6.6 %collective-permute-done.18 = bf16[2,64,1332]{2,1,0:T(8,128)(2,1)S(1)} collective-permute-done((bf16[2,64,1332]{2,1,0:T(8,128)(2,1)S(1)}, bf16[2,64,1332]{2,1,0:T(8,128)(2,1)S(1)}, u32[]{:S(2)}, u32[]{:S(2)}) %collective-permute-start.18) | collective-permute-done | bytes 341024 | tf_op jit(solution)/shard_map/ppermute | solution.py:298
  164.4 3.4 collective-permute-done.21
  168.0 6.1 %convolution_convert_fusion.8 = bf16[256,1332]{0,1:T(8,128)(2,1)} fusion(bf16[256,2664]{1,0:T(8,128)(2,1)S(1)} %bitcast.344, bf16[1332,2664]{1,0:T(8,128)(2,1)} %param.11), kind=kOutput, calls=%fused_computation.20 | convolution fusion | flops 1817146368 | bytes 9142848 | tf_op jit(solution)/shard_map/dot_general | solution.py:301
  177.6 4.8 collective-permute-done.25
  182.4 3.7 collective-permute-start.20
  186.4 3.8 collective-permute-start.27
  190.3 2.1 collective-permute-start.26
  193.2 7.6 %collective-permute-done.26 = bf16[64,1332]{1,0:T(8,128)(2,1)S(1)} collective-permute-done((bf16[64,1332]{1,0:T(8,128)(2,1)S(1)}, bf16[64,1332]{1,0:T(8,128)(2,1)S(1)}, u32[]{:S(2)}, u32[]{:S(2)}) %collective-permute-start.26) | collective-permute-done | bytes 170528 | tf_op jit(solution)/shard_map/ppermute | solution.py:295
  201.4 2.0 collective-permute-done.27
  207.3 73.1 %shard_map.109 = bf16[4,64,2664]{2,1,0:T(8,128)(2,1)} custom-call(s32[89]{0:T(128)} %pad_add_fusion.scalar_ref, bf16[8,64,1332]{2,1,0:T(8,128)(2,1)} %bitcast_dynamic-update-slice_fusion.7.x_ref, f32[5,2,152,128]{3,2,1,0:T(8,128)} %copy.38.con_ref, bf16[80,144,160]{2,1,0:T(8,128)(2,1)} %constant.71.clone.synth_ref, ...), custom_call_target="tpu_custom_call" | custom-call | flops 1571291136 | bytes 16777216 | tf_op jit(solution)/shard_map/pallas_call | solution.py:239
  283.7 8.5 %collective-permute-done.32 = bf16[64,2664]{1,0:T(8,128)(2,1)S(1)} collective-permute-done((bf16[64,2664]{1,0:T(8,128)(2,1)S(1)}, bf16[64,2664]{1,0:T(8,128)(2,1)S(1)}, u32[]{:S(2)}, u32[]{:S(2)}) %collective-permute-start.32) | collective-permute-done | bytes 341024 | tf_op jit(solution)/shard_map/ppermute | solution.py:298
  292.2 6.9 %collective-permute-done.31 = bf16[64,2664]{1,0:T(8,128)(2,1)S(1)} collective-permute-done((bf16[64,2664]{1,0:T(8,128)(2,1)S(1)}, bf16[64,2664]{1,0:T(8,128)(2,1)S(1)}, u32[]{:S(2)}, u32[]{:S(2)}) %collective-permute-start.31) | collective-permute-done | bytes 341024 | tf_op jit(solution)/shard_map/ppermute | solution.py:298
  301.8 2.9 collective-permute-start.37
  304.7 2.2 collective-permute-start.36
  307.3 3.1 convolution_convert_fusion.7
  314.6 22.6 %collective-permute-done.37 = bf16[4,64,2664]{2,1,0:T(8,128)(2,1)S(1)} collective-permute-done((bf16[4,64,2664]{2,1,0:T(8,128)(2,1)}, bf16[4,64,2664]{2,1,0:T(8,128)(2,1)S(1)}, u32[]{:S(2)}, u32[]{:S(2)}) %collective-permute-start.37) | collective-permute-done | bytes 1364000 | tf_op jit(solution)/shard_map/ppermute | solution.py:295
  340.5 8.4 %convolution_convert_fusion.2 = bf16[512,1332]{0,1:T(8,128)(2,1)} fusion(bf16[512,2664]{1,0:T(8,128)(2,1)S(1)} %bitcast.335, bf16[1332,2664]{1,0:T(8,128)(2,1)} %param.11), kind=kOutput, calls=%fused_computation.4 | convolution fusion | flops 3634292736 | bytes 11188800 | tf_op jit(solution)/shard_map/dot_general | solution.py:301
  348.9 1.8 copy.40
  352.7 2.3 collective-permute-start.43
  356.8 4.8 collective-permute-done.40
  361.5 6.2 %collective-permute-done.39 = bf16[2,64,1332]{2,1,0:T(8,128)(2,1)S(1)} collective-permute-done((bf16[2,64,1332]{2,1,0:T(8,128)(2,1)S(1)}, bf16[2,64,1332]{2,1,0:T(8,128)(2,1)S(1)}, u32[]{:S(2)}, u32[]{:S(2)}) %collective-permute-start.39) | collective-permute-done | bytes 341024 | tf_op jit(solution)/shard_map/ppermute | solution.py:298
  368.7 2.3 collective-permute-start.41
  371.0 14.8 %collective-permute-done.43 = bf16[4,64,2664]{2,1,0:T(8,128)(2,1)S(1)} collective-permute-done((bf16[4,64,2664]{2,1,0:T(8,128)(2,1)S(1)}, bf16[4,64,2664]{2,1,0:T(8,128)(2,1)S(1)}, u32[]{:S(2)}, u32[]{:S(2)}) %collective-permute-start.43) | collective-permute-done | bytes 1364000 | tf_op jit(solution)/shard_map/ppermute | solution.py:295
  388.2 7.2 %convolution_convert_fusion.1 = bf16[512,1332]{0,1:T(8,128)(2,1)S(1)} fusion(bf16[512,2664]{1,0:T(8,128)(2,1)S(1)} %bitcast.336, bf16[1332,2664]{1,0:T(8,128)(2,1)} %param.11), kind=kOutput, calls=%fused_computation.3 | convolution fusion | flops 3634292736 | bytes 11188800 | tf_op jit(solution)/shard_map/dot_general | solution.py:301
  401.8 5.2 collective-permute-done.46
  407.0 6.2 %collective-permute-done.45 = bf16[2,64,1332]{2,1,0:T(8,128)(2,1)S(1)} collective-permute-done((bf16[2,64,1332]{2,1,0:T(8,128)(2,1)S(1)}, bf16[2,64,1332]{2,1,0:T(8,128)(2,1)S(1)}, u32[]{:S(2)}, u32[]{:S(2)}) %collective-permute-start.45) | collective-permute-done | bytes 341024 | tf_op jit(solution)/shard_map/ppermute | solution.py:298
  414.2 2.4 collective-permute-start.47
  416.6 15.4 %collective-permute-done.49 = bf16[4,64,2664]{2,1,0:T(8,128)(2,1)S(1)} collective-permute-done((bf16[4,64,2664]{2,1,0:T(8,128)(2,1)S(1)}, bf16[4,64,2664]{2,1,0:T(8,128)(2,1)S(1)}, u32[]{:S(2)}, u32[]{:S(2)}) %collective-permute-start.49) | collective-permute-done | bytes 1364000 | tf_op jit(solution)/shard_map/ppermute | solution.py:295
  433.1 8.3 %convolution_convert_fusion = bf16[512,1332]{0,1:T(8,128)(2,1)} fusion(bf16[512,2664]{1,0:T(8,128)(2,1)S(1)} %bitcast.337, bf16[1332,2664]{1,0:T(8,128)(2,1)} %param.11), kind=kOutput, calls=%fused_computation.2 | convolution fusion | flops 3634292736 | bytes 11188800 | tf_op jit(solution)/shard_map/dot_general | solution.py:301
  446.8 2.1 collective-permute-start.54
  450.5 3.6 collective-permute-done.52
  454.1 3.4 collective-permute-start.62
  457.5 2.9 collective-permute-done.51
  460.4 2.2 collective-permute-start.61
  465.3 5.3 convolution_convert_fusion.6
  472.9 5.0 collective-permute-done.58
  480.3 2.8 collective-permute-start.60
  483.2 2.9 collective-permute-start.59
  486.8 7.7 %collective-permute-done.59 = bf16[64,1332]{1,0:T(8,128)(2,1)S(1)} collective-permute-done((bf16[64,1332]{1,0:T(8,128)(2,1)S(1)}, bf16[64,1332]{1,0:T(8,128)(2,1)S(1)}, u32[]{:S(2)}, u32[]{:S(2)}) %collective-permute-start.59) | collective-permute-done | bytes 170528 | tf_op jit(solution)/shard_map/ppermute | solution.py:295
  495.1 3.1 collective-permute-done.60
  502.2 73.2 %shard_map.110 = bf16[4,64,2664]{2,1,0:T(8,128)(2,1)} custom-call(s32[89]{0:T(128)} %pad_add_fusion.scalar_ref, bf16[8,64,1332]{2,1,0:T(8,128)(2,1)} %bitcast_dynamic-update-slice_fusion.x_ref, f32[5,2,152,128]{3,2,1,0:T(8,128)} %copy.38.con_ref, bf16[80,144,160]{2,1,0:T(8,128)(2,1)} %constant.71.clone.synth_ref, ...), custom_call_target="tpu_custom_call" | custom-call | flops 1571291136 | bytes 16777216 | tf_op jit(solution)/shard_map/pallas_call | solution.py:239
  578.7 8.3 %collective-permute-done.65 = bf16[64,2664]{1,0:T(8,128)(2,1)S(1)} collective-permute-done((bf16[64,2664]{1,0:T(8,128)(2,1)S(1)}, bf16[64,2664]{1,0:T(8,128)(2,1)S(1)}, u32[]{:S(2)}, u32[]{:S(2)}) %collective-permute-start.65) | collective-permute-done | bytes 341024 | tf_op jit(solution)/shard_map/ppermute | solution.py:298
  587.0 7.6 %collective-permute-done.64 = bf16[64,2664]{1,0:T(8,128)(2,1)S(1)} collective-permute-done((bf16[64,2664]{1,0:T(8,128)(2,1)S(1)}, bf16[64,2664]{1,0:T(8,128)(2,1)S(1)}, u32[]{:S(2)}, u32[]{:S(2)}) %collective-permute-start.64) | collective-permute-done | bytes 341024 | tf_op jit(solution)/shard_map/ppermute | solution.py:298
  (224 shorter events, 101.1 us)
Async XLA Ops:
  2.7 33.3 %collective-permute-start.4 = (bf16[4,64,2664]{2,1,0:T(8,128)(2,1)S(1)}, bf16[4,64,2664]{2,1,0:T(8,128)(2,1)}, u32[]{:S(2)}, u32[]{:S(2)}) collective-permute-start(bf16[4,64,2664]{2,1,0:T(8,128)(2,1)S(1)} %pad_maximum_fusion.6), channel_id=1, source_target_pairs={{8,0},{16,8},{24,16},{28,24},{20,28},{12,20},{4,12},{0,4},{9,1},{1... | collective-permute-start | bytes 4091912 | tf_op jit(solution)/shard_map/ppermute | solution.py:295
  5.6 31.8 %collective-permute-start.3 = (bf16[4,64,2664]{2,1,0:T(8,128)(2,1)S(1)}, bf16[4,64,2664]{2,1,0:T(8,128)(2,1)}, u32[]{:S(2)}, u32[]{:S(2)}) collective-permute-start(bf16[4,64,2664]{2,1,0:T(8,128)(2,1)S(1)} %pad_maximum_fusion.6), channel_id=1, source_target_pairs={{8,16},{16,24},{24,28},{28,20},{20,12},{12,4},{4,0},{0,8},{9,17},{... | collective-permute-start | bytes 4091912 | tf_op jit(solution)/shard_map/ppermute | solution.py:295
  12.3 39.1 %collective-permute-start.2 = (bf16[1,64,1332]{2,1,0:T(8,128)(2,1)}, bf16[1,64,1332]{2,1,0:T(8,128)(2,1)}, u32[]{:S(2)}, u32[]{:S(2)}) collective-permute-start(bf16[1,64,1332]{2,1,0:T(8,128)(2,1)} %get-tuple-element.49), channel_id=1, source_target_pairs={{0,3},{1,2},{2,1},{3,0},{4,7},{5,6},{6,5},{7,4},{8,11},{9,10},{10,... | collective-permute-start | bytes 511496 | tf_op jit(solution)/shard_map/ppermute | solution.py:298
  13.0 38.6 %collective-permute-start.1 = (bf16[1,64,1332]{2,1,0:T(8,128)(2,1)}, bf16[1,64,1332]{2,1,0:T(8,128)(2,1)}, u32[]{:S(2)}, u32[]{:S(2)}) collective-permute-start(bf16[1,64,1332]{2,1,0:T(8,128)(2,1)} %get-tuple-element.50), channel_id=1, source_target_pairs={{0,2},{1,3},{2,0},{3,1},{4,6},{5,7},{6,4},{7,5},{8,10},{9,11},{10,... | collective-permute-start | bytes 511496 | tf_op jit(solution)/shard_map/ppermute | solution.py:298
  14.1 39.1 %collective-permute-start = (bf16[1,64,1332]{2,1,0:T(8,128)(2,1)}, bf16[1,64,1332]{2,1,0:T(8,128)(2,1)}, u32[]{:S(2)}, u32[]{:S(2)}) collective-permute-start(bf16[1,64,1332]{2,1,0:T(8,128)(2,1)} %get-tuple-element.48), channel_id=1, source_target_pairs={{0,1},{1,0},{2,3},{3,2},{4,5},{5,4},{6,7},{7,6},{8,9},{9,8},{10,11... | collective-permute-start | bytes 511496 | tf_op jit(solution)/shard_map/ppermute | solution.py:298
  49.7 10.7 %collective-permute-start.7 = (bf16[2,64,1332]{2,1,0:T(8,128)(2,1)S(1)}, bf16[2,64,1332]{2,1,0:T(8,128)(2,1)S(1)}, u32[]{:S(2)}, u32[]{:S(2)}) collective-permute-start(bf16[2,64,1332]{2,1,0:T(8,128)(2,1)S(1)} %get-tuple-element.22), channel_id=1, source_target_pairs={{0,3},{1,2},{2,1},{3,0},{4,7},{5,6},{6,5},{7,4},{8,11},{9,10},{10,... | collective-permute-start | bytes 1022984 | tf_op jit(solution)/shard_map/ppermute | solution.py:298
  49.8 18.4 %collective-permute-start.6 = (bf16[2,64,1332]{2,1,0:T(8,128)(2,1)S(1)}, bf16[2,64,1332]{2,1,0:T(8,128)(2,1)S(1)}, u32[]{:S(2)}, u32[]{:S(2)}) collective-permute-start(bf16[2,64,1332]{2,1,0:T(8,128)(2,1)S(1)} %get-tuple-element.21), channel_id=1, source_target_pairs={{0,2},{1,3},{2,0},{3,1},{4,6},{5,7},{6,4},{7,5},{8,10},{9,11},{10,... | collective-permute-start | bytes 1022984 | tf_op jit(solution)/shard_map/ppermute | solution.py:298
  51.4 16.8 %collective-permute-start.5 = (bf16[2,64,1332]{2,1,0:T(8,128)(2,1)S(1)}, bf16[2,64,1332]{2,1,0:T(8,128)(2,1)S(1)}, u32[]{:S(2)}, u32[]{:S(2)}) collective-permute-start(bf16[2,64,1332]{2,1,0:T(8,128)(2,1)S(1)} %get-tuple-element.20), channel_id=1, source_target_pairs={{0,1},{1,0},{2,3},{3,2},{4,5},{5,4},{6,7},{7,6},{8,9},{9,8},{10,11... | collective-permute-start | bytes 1022984 | tf_op jit(solution)/shard_map/ppermute | solution.py:298
  51.6 33.3 %collective-permute-start.10 = (bf16[4,64,2664]{2,1,0:T(8,128)(2,1)}, bf16[4,64,2664]{2,1,0:T(8,128)(2,1)S(1)}, u32[]{:S(2)}, u32[]{:S(2)}) collective-permute-start(bf16[4,64,2664]{2,1,0:T(8,128)(2,1)} %collective-permute-done.4), channel_id=1, source_target_pairs={{8,0},{16,8},{24,16},{28,24},{20,28},{12,20},{4,12},{0,4},{9,1},{1... | collective-permute-start | bytes 4091912 | tf_op jit(solution)/shard_map/ppermute | solution.py:295
  53.2 32.3 %collective-permute-start.9 = (bf16[4,64,2664]{2,1,0:T(8,128)(2,1)}, bf16[4,64,2664]{2,1,0:T(8,128)(2,1)S(1)}, u32[]{:S(2)}, u32[]{:S(2)}) collective-permute-start(bf16[4,64,2664]{2,1,0:T(8,128)(2,1)} %collective-permute-done.3), channel_id=1, source_target_pairs={{8,16},{16,24},{24,28},{28,20},{20,12},{12,4},{4,0},{0,8},{9,17},{... | collective-permute-start | bytes 4091912 | tf_op jit(solution)/shard_map/ppermute | solution.py:295
  69.2 31.2 %collective-permute-start.8 = (bf16[64,1332]{1,0:T(8,128)(2,1)}, bf16[64,1332]{1,0:T(8,128)(2,1)}, u32[]{:S(2)}, u32[]{:S(2)}) collective-permute-start(bf16[64,1332]{1,0:T(8,128)(2,1)} %get-tuple-element.58), channel_id=1, source_target_pairs={{8,0},{16,8},{24,16},{28,24},{20,28},{12,20},{4,12},{0,4},{9,1},{1... | collective-permute-start | bytes 511496 | tf_op jit(solution)/shard_map/ppermute | solution.py:295
  96.8 10.8 %collective-permute-start.13 = (bf16[2,64,1332]{2,1,0:T(8,128)(2,1)S(1)}, bf16[2,64,1332]{2,1,0:T(8,128)(2,1)S(1)}, u32[]{:S(2)}, u32[]{:S(2)}) collective-permute-start(bf16[2,64,1332]{2,1,0:T(8,128)(2,1)S(1)} %get-tuple-element.19), channel_id=1, source_target_pairs={{0,3},{1,2},{2,1},{3,0},{4,7},{5,6},{6,5},{7,4},{8,11},{9,10},{10,... | collective-permute-start | bytes 1022984 | tf_op jit(solution)/shard_map/ppermute | solution.py:298
  96.9 18.3 %collective-permute-start.12 = (bf16[2,64,1332]{2,1,0:T(8,128)(2,1)S(1)}, bf16[2,64,1332]{2,1,0:T(8,128)(2,1)S(1)}, u32[]{:S(2)}, u32[]{:S(2)}) collective-permute-start(bf16[2,64,1332]{2,1,0:T(8,128)(2,1)S(1)} %get-tuple-element.18), channel_id=1, source_target_pairs={{0,2},{1,3},{2,0},{3,1},{4,6},{5,7},{6,4},{7,5},{8,10},{9,11},{10,... | collective-permute-start | bytes 1022984 | tf_op jit(solution)/shard_map/ppermute | solution.py:298
  98.4 16.9 %collective-permute-start.11 = (bf16[2,64,1332]{2,1,0:T(8,128)(2,1)S(1)}, bf16[2,64,1332]{2,1,0:T(8,128)(2,1)S(1)}, u32[]{:S(2)}, u32[]{:S(2)}) collective-permute-start(bf16[2,64,1332]{2,1,0:T(8,128)(2,1)S(1)} %get-tuple-element.17), channel_id=1, source_target_pairs={{0,1},{1,0},{2,3},{3,2},{4,5},{5,4},{6,7},{7,6},{8,9},{9,8},{10,11... | collective-permute-start | bytes 1022984 | tf_op jit(solution)/shard_map/ppermute | solution.py:298
  98.7 34.2 %collective-permute-start.16 = (bf16[4,64,2664]{2,1,0:T(8,128)(2,1)S(1)}, bf16[4,64,2664]{2,1,0:T(8,128)(2,1)S(1)}, u32[]{:S(2)}, u32[]{:S(2)}) collective-permute-start(bf16[4,64,2664]{2,1,0:T(8,128)(2,1)S(1)} %copy-done.15), channel_id=1, source_target_pairs={{8,0},{16,8},{24,16},{28,24},{20,28},{12,20},{4,12},{0,4},{9,1},{1... | collective-permute-start | bytes 4091912 | tf_op jit(solution)/shard_map/ppermute | solution.py:295
  100.3 32.6 %collective-permute-start.15 = (bf16[4,64,2664]{2,1,0:T(8,128)(2,1)}, bf16[4,64,2664]{2,1,0:T(8,128)(2,1)S(1)}, u32[]{:S(2)}, u32[]{:S(2)}) collective-permute-start(bf16[4,64,2664]{2,1,0:T(8,128)(2,1)} %copy-done.20), channel_id=1, source_target_pairs={{8,16},{16,24},{24,28},{28,20},{20,12},{12,4},{4,0},{0,8},{9,17},{... | collective-permute-start | bytes 4091912 | tf_op jit(solution)/shard_map/ppermute | solution.py:295
  116.2 31.5 %collective-permute-start.14 = (bf16[64,1332]{1,0:T(8,128)(2,1)}, bf16[64,1332]{1,0:T(8,128)(2,1)}, u32[]{:S(2)}, u32[]{:S(2)}) collective-permute-start(bf16[64,1332]{1,0:T(8,128)(2,1)} %get-tuple-element.60), channel_id=1, source_target_pairs={{8,4},{16,0},{24,8},{28,16},{20,24},{12,28},{4,20},{0,12},{9,5},{1... | collective-permute-start | bytes 511496 | tf_op jit(solution)/shard_map/ppermute | solution.py:295
  144.7 10.8 %collective-permute-start.19 = (bf16[2,64,1332]{2,1,0:T(8,128)(2,1)S(1)}, bf16[2,64,1332]{2,1,0:T(8,128)(2,1)S(1)}, u32[]{:S(2)}, u32[]{:S(2)}) collective-permute-start(bf16[2,64,1332]{2,1,0:T(8,128)(2,1)S(1)} %get-tuple-element.16), channel_id=1, source_target_pairs={{0,3},{1,2},{2,1},{3,0},{4,7},{5,6},{6,5},{7,4},{8,11},{9,10},{10,... | collective-permute-start | bytes 1022984 | tf_op jit(solution)/shard_map/ppermute | solution.py:298
  144.8 18.1 %collective-permute-start.18 = (bf16[2,64,1332]{2,1,0:T(8,128)(2,1)S(1)}, bf16[2,64,1332]{2,1,0:T(8,128)(2,1)S(1)}, u32[]{:S(2)}, u32[]{:S(2)}) collective-permute-start(bf16[2,64,1332]{2,1,0:T(8,128)(2,1)S(1)} %get-tuple-element.15), channel_id=1, source_target_pairs={{0,2},{1,3},{2,0},{3,1},{4,6},{5,7},{6,4},{7,5},{8,10},{9,11},{10,... | collective-permute-start | bytes 1022984 | tf_op jit(solution)/shard_map/ppermute | solution.py:298
  146.2 17.4 %collective-permute-start.17 = (bf16[2,64,1332]{2,1,0:T(8,128)(2,1)S(1)}, bf16[2,64,1332]{2,1,0:T(8,128)(2,1)S(1)}, u32[]{:S(2)}, u32[]{:S(2)}) collective-permute-start(bf16[2,64,1332]{2,1,0:T(8,128)(2,1)S(1)} %get-tuple-element.14), channel_id=1, source_target_pairs={{0,1},{1,0},{2,3},{3,2},{4,5},{5,4},{6,7},{7,6},{8,9},{9,8},{10,11... | collective-permute-start | bytes 1022984 | tf_op jit(solution)/shard_map/ppermute | solution.py:298
  146.7 17.7 %collective-permute-start.22 = (bf16[4,32,2664]{2,1,0:T(8,128)(2,1)S(1)}, bf16[4,32,2664]{2,1,0:T(8,128)(2,1)S(1)}, u32[]{:S(2)}, u32[]{:S(2)}) collective-permute-start(bf16[4,32,2664]{2,1,0:T(8,128)(2,1)S(1)} %slice.285), channel_id=1, source_target_pairs={{8,0},{16,8},{24,16},{28,24},{20,28},{12,20},{4,12},{0,4},{9,1},{1... | collective-permute-start | bytes 2045960 | tf_op jit(solution)/shard_map/ppermute | solution.py:295
  147.7 20.2 %collective-permute-start.21 = (bf16[4,32,2664]{2,1,0:T(8,128)(2,1)S(1)}, bf16[4,32,2664]{2,1,0:T(8,128)(2,1)S(1)}, u32[]{:S(2)}, u32[]{:S(2)}) collective-permute-start(bf16[4,32,2664]{2,1,0:T(8,128)(2,1)S(1)} %slice.284), channel_id=1, source_target_pairs={{8,16},{16,24},{24,28},{28,20},{20,12},{12,4},{4,0},{0,8},{9,17},{... | collective-permute-start | bytes 2045960 | tf_op jit(solution)/shard_map/ppermute | solution.py:295
  155.5 50.2 %collective-permute-start.29 = (bf16[64,1332]{1,0:T(8,128)(2,1)}, bf16[64,1332]{1,0:T(8,128)(2,1)}, u32[]{:S(2)}, u32[]{:S(2)}) collective-permute-start(bf16[64,1332]{1,0:T(8,128)(2,1)} %get-tuple-element.57), channel_id=1, source_target_pairs={{8,16},{16,24},{24,28},{28,20},{20,12},{12,4},{4,0},{0,8},{9,17},{... | collective-permute-start | bytes 511496 | tf_op jit(solution)/shard_map/ppermute | solution.py:295
  162.9 41.1 %collective-permute-start.28 = (bf16[64,1332]{1,0:T(8,128)(2,1)}, bf16[64,1332]{1,0:T(8,128)(2,1)}, u32[]{:S(2)}, u32[]{:S(2)}) collective-permute-start(bf16[64,1332]{1,0:T(8,128)(2,1)} %get-tuple-element.59), channel_id=1, source_target_pairs={{8,24},{16,28},{24,20},{28,12},{20,4},{12,0},{4,8},{0,16},{9,25},{... | collective-permute-start | bytes 511496 | tf_op jit(solution)/shard_map/ppermute | solution.py:295
  175.7 10.7 %collective-permute-start.24 = (bf16[1,64,1332]{2,1,0:T(8,128)(2,1)S(1)}, bf16[1,64,1332]{2,1,0:T(8,128)(2,1)S(1)}, u32[]{:S(2)}, u32[]{:S(2)}) collective-permute-start(bf16[1,64,1332]{2,1,0:T(8,128)(2,1)S(1)} %get-tuple-element.47), channel_id=1, source_target_pairs={{0,2},{1,3},{2,0},{3,1},{4,6},{5,7},{6,4},{7,5},{8,10},{9,11},{10,... | collective-permute-start | bytes 511496 | tf_op jit(solution)/shard_map/ppermute | solution.py:298
  177.4 12.8 %collective-permute-start.23 = (bf16[1,64,1332]{2,1,0:T(8,128)(2,1)S(1)}, bf16[1,64,1332]{2,1,0:T(8,128)(2,1)S(1)}, u32[]{:S(2)}, u32[]{:S(2)}) collective-permute-start(bf16[1,64,1332]{2,1,0:T(8,128)(2,1)S(1)} %get-tuple-element.45), channel_id=1, source_target_pairs={{0,1},{1,0},{2,3},{3,2},{4,5},{5,4},{6,7},{7,6},{8,9},{9,8},{10,11... | collective-permute-start | bytes 511496 | tf_op jit(solution)/shard_map/ppermute | solution.py:298
  182.4 10.1 %collective-permute-start.20 = (bf16[64,1332]{1,0:T(8,128)(2,1)S(1)}, bf16[64,1332]{1,0:T(8,128)(2,1)S(1)}, u32[]{:S(2)}, u32[]{:S(2)}) collective-permute-start(bf16[64,1332]{1,0:T(8,128)(2,1)S(1)} %get-tuple-element.62), channel_id=1, source_target_pairs={{8,12},{16,4},{24,0},{28,8},{20,16},{12,24},{4,28},{0,20},{9,13},{... | collective-permute-start | bytes 511496 | tf_op jit(solution)/shard_map/ppermute | solution.py:295
  186.4 16.9 %collective-permute-start.27 = (bf16[64,1332]{1,0:T(8,128)(2,1)S(1)}, bf16[64,1332]{1,0:T(8,128)(2,1)S(1)}, u32[]{:S(2)}, u32[]{:S(2)}) collective-permute-start(bf16[64,1332]{1,0:T(8,128)(2,1)S(1)} %get-tuple-element.61), channel_id=1, source_target_pairs={{8,28},{16,20},{24,12},{28,4},{20,0},{12,8},{4,16},{0,24},{9,29},{... | collective-permute-start | bytes 511496 | tf_op jit(solution)/shard_map/ppermute | solution.py:295
  190.3 10.4 %collective-permute-start.26 = (bf16[64,1332]{1,0:T(8,128)(2,1)S(1)}, bf16[64,1332]{1,0:T(8,128)(2,1)S(1)}, u32[]{:S(2)}, u32[]{:S(2)}) collective-permute-start(bf16[64,1332]{1,0:T(8,128)(2,1)S(1)} %fusion.35), channel_id=1, source_target_pairs={{8,20},{16,12},{24,4},{28,0},{20,8},{12,16},{4,24},{0,28},{9,21},{... | collective-permute-start | bytes 511496 | tf_op jit(solution)/shard_map/ppermute | solution.py:295
  281.8 10.4 %collective-permute-start.32 = (bf16[64,2664]{1,0:T(8,128)(2,1)S(1)}, bf16[64,2664]{1,0:T(8,128)(2,1)S(1)}, u32[]{:S(2)}, u32[]{:S(2)}) collective-permute-start(bf16[64,2664]{1,0:T(8,128)(2,1)S(1)} %get-tuple-element.32), channel_id=1, source_target_pairs={{0,3},{1,2},{2,1},{3,0},{4,7},{5,6},{6,5},{7,4},{8,11},{9,10},{10,... | collective-permute-start | bytes 1022984 | tf_op jit(solution)/shard_map/ppermute | solution.py:298
  281.9 17.2 %collective-permute-start.31 = (bf16[64,2664]{1,0:T(8,128)(2,1)S(1)}, bf16[64,2664]{1,0:T(8,128)(2,1)S(1)}, u32[]{:S(2)}, u32[]{:S(2)}) collective-permute-start(bf16[64,2664]{1,0:T(8,128)(2,1)S(1)} %get-tuple-element.33), channel_id=1, source_target_pairs={{0,2},{1,3},{2,0},{3,1},{4,6},{5,7},{6,4},{7,5},{8,10},{9,11},{10,... | collective-permute-start | bytes 1022984 | tf_op jit(solution)/shard_map/ppermute | solution.py:298
  283.1 16.0 %collective-permute-start.30 = (bf16[64,2664]{1,0:T(8,128)(2,1)S(1)}, bf16[64,2664]{1,0:T(8,128)(2,1)S(1)}, u32[]{:S(2)}, u32[]{:S(2)}) collective-permute-start(bf16[64,2664]{1,0:T(8,128)(2,1)S(1)} %get-tuple-element.34), channel_id=1, source_target_pairs={{0,1},{1,0},{2,3},{3,2},{4,5},{5,4},{6,7},{7,6},{8,9},{9,8},{10,11... | collective-permute-start | bytes 1022984 | tf_op jit(solution)/shard_map/ppermute | solution.py:298
  301.8 35.3 %collective-permute-start.37 = (bf16[4,64,2664]{2,1,0:T(8,128)(2,1)}, bf16[4,64,2664]{2,1,0:T(8,128)(2,1)S(1)}, u32[]{:S(2)}, u32[]{:S(2)}) collective-permute-start(bf16[4,64,2664]{2,1,0:T(8,128)(2,1)} %fusion), channel_id=1, source_target_pairs={{8,0},{16,8},{24,16},{28,24},{20,28},{12,20},{4,12},{0,4},{9,1},{1... | collective-permute-start | bytes 4091912 | tf_op jit(solution)/shard_map/ppermute | solution.py:295
  304.7 34.1 %collective-permute-start.36 = (bf16[4,64,2664]{2,1,0:T(8,128)(2,1)}, bf16[4,64,2664]{2,1,0:T(8,128)(2,1)}, u32[]{:S(2)}, u32[]{:S(2)}) collective-permute-start(bf16[4,64,2664]{2,1,0:T(8,128)(2,1)} %fusion), channel_id=1, source_target_pairs={{8,16},{16,24},{24,28},{28,20},{20,12},{12,4},{4,0},{0,8},{9,17},{... | collective-permute-start | bytes 4091912 | tf_op jit(solution)/shard_map/ppermute | solution.py:295
  312.7 38.8 %collective-permute-start.35 = (bf16[1,64,1332]{2,1,0:T(8,128)(2,1)}, bf16[1,64,1332]{2,1,0:T(8,128)(2,1)S(1)}, u32[]{:S(2)}, u32[]{:S(2)}) collective-permute-start(bf16[1,64,1332]{2,1,0:T(8,128)(2,1)} %get-tuple-element.43), channel_id=1, source_target_pairs={{0,3},{1,2},{2,1},{3,0},{4,7},{5,6},{6,5},{7,4},{8,11},{9,10},{10,... | collective-permute-start | bytes 511496 | tf_op jit(solution)/shard_map/ppermute | solution.py:298
  312.7 40.0 %collective-permute-start.34 = (bf16[1,64,1332]{2,1,0:T(8,128)(2,1)}, bf16[1,64,1332]{2,1,0:T(8,128)(2,1)}, u32[]{:S(2)}, u32[]{:S(2)}) collective-permute-start(bf16[1,64,1332]{2,1,0:T(8,128)(2,1)} %get-tuple-element.44), channel_id=1, source_target_pairs={{0,2},{1,3},{2,0},{3,1},{4,6},{5,7},{6,4},{7,5},{8,10},{9,11},{10,... | collective-permute-start | bytes 511496 | tf_op jit(solution)/shard_map/ppermute | solution.py:298
  314.0 41.0 %collective-permute-start.33 = (bf16[1,64,1332]{2,1,0:T(8,128)(2,1)}, bf16[1,64,1332]{2,1,0:T(8,128)(2,1)}, u32[]{:S(2)}, u32[]{:S(2)}) collective-permute-start(bf16[1,64,1332]{2,1,0:T(8,128)(2,1)} %get-tuple-element.42), channel_id=1, source_target_pairs={{0,1},{1,0},{2,3},{3,2},{4,5},{5,4},{6,7},{7,6},{8,9},{9,8},{10,11... | collective-permute-start | bytes 511496 | tf_op jit(solution)/shard_map/ppermute | solution.py:298
  350.8 10.8 %collective-permute-start.40 = (bf16[2,64,1332]{2,1,0:T(8,128)(2,1)S(1)}, bf16[2,64,1332]{2,1,0:T(8,128)(2,1)S(1)}, u32[]{:S(2)}, u32[]{:S(2)}) collective-permute-start(bf16[2,64,1332]{2,1,0:T(8,128)(2,1)S(1)} %get-tuple-element.13), channel_id=1, source_target_pairs={{0,3},{1,2},{2,1},{3,0},{4,7},{5,6},{6,5},{7,4},{8,11},{9,10},{10,... | collective-permute-start | bytes 1022984 | tf_op jit(solution)/shard_map/ppermute | solution.py:298
  350.8 16.9 %collective-permute-start.39 = (bf16[2,64,1332]{2,1,0:T(8,128)(2,1)S(1)}, bf16[2,64,1332]{2,1,0:T(8,128)(2,1)S(1)}, u32[]{:S(2)}, u32[]{:S(2)}) collective-permute-start(bf16[2,64,1332]{2,1,0:T(8,128)(2,1)S(1)} %get-tuple-element.12), channel_id=1, source_target_pairs={{0,2},{1,3},{2,0},{3,1},{4,6},{5,7},{6,4},{7,5},{8,10},{9,11},{10,... | collective-permute-start | bytes 1022984 | tf_op jit(solution)/shard_map/ppermute | solution.py:298
  351.5 16.2 %collective-permute-start.38 = (bf16[2,64,1332]{2,1,0:T(8,128)(2,1)S(1)}, bf16[2,64,1332]{2,1,0:T(8,128)(2,1)S(1)}, u32[]{:S(2)}, u32[]{:S(2)}) collective-permute-start(bf16[2,64,1332]{2,1,0:T(8,128)(2,1)S(1)} %get-tuple-element.11), channel_id=1, source_target_pairs={{0,1},{1,0},{2,3},{3,2},{4,5},{5,4},{6,7},{7,6},{8,9},{9,8},{10,11... | collective-permute-start | bytes 1022984 | tf_op jit(solution)/shard_map/ppermute | solution.py:298
  352.7 33.1 %collective-permute-start.43 = (bf16[4,64,2664]{2,1,0:T(8,128)(2,1)S(1)}, bf16[4,64,2664]{2,1,0:T(8,128)(2,1)S(1)}, u32[]{:S(2)}, u32[]{:S(2)}) collective-permute-start(bf16[4,64,2664]{2,1,0:T(8,128)(2,1)S(1)} %copy-done.19), channel_id=1, source_target_pairs={{8,0},{16,8},{24,16},{28,24},{20,28},{12,20},{4,12},{0,4},{9,1},{1... | collective-permute-start | bytes 4091912 | tf_op jit(solution)/shard_map/ppermute | solution.py:295
  355.0 32.1 %collective-permute-start.42 = (bf16[4,64,2664]{2,1,0:T(8,128)(2,1)}, bf16[4,64,2664]{2,1,0:T(8,128)(2,1)S(1)}, u32[]{:S(2)}, u32[]{:S(2)}) collective-permute-start(bf16[4,64,2664]{2,1,0:T(8,128)(2,1)} %collective-permute-done.36), channel_id=1, source_target_pairs={{8,16},{16,24},{24,28},{28,20},{20,12},{12,4},{4,0},{0,8},{9,17},{... | collective-permute-start | bytes 4091912 | tf_op jit(solution)/shard_map/ppermute | solution.py:295
  368.7 31.2 %collective-permute-start.41 = (bf16[64,1332]{1,0:T(8,128)(2,1)}, bf16[64,1332]{1,0:T(8,128)(2,1)}, u32[]{:S(2)}, u32[]{:S(2)}) collective-permute-start(bf16[64,1332]{1,0:T(8,128)(2,1)} %get-tuple-element.52), channel_id=1, source_target_pairs={{8,0},{16,8},{24,16},{28,24},{20,28},{12,20},{4,12},{0,4},{9,1},{1... | collective-permute-start | bytes 511496 | tf_op jit(solution)/shard_map/ppermute | solution.py:295
  396.3 10.8 %collective-permute-start.46 = (bf16[2,64,1332]{2,1,0:T(8,128)(2,1)S(1)}, bf16[2,64,1332]{2,1,0:T(8,128)(2,1)S(1)}, u32[]{:S(2)}, u32[]{:S(2)}) collective-permute-start(bf16[2,64,1332]{2,1,0:T(8,128)(2,1)S(1)} %get-tuple-element.10), channel_id=1, source_target_pairs={{0,3},{1,2},{2,1},{3,0},{4,7},{5,6},{6,5},{7,4},{8,11},{9,10},{10,... | collective-permute-start | bytes 1022984 | tf_op jit(solution)/shard_map/ppermute | solution.py:298
  396.3 16.9 %collective-permute-start.45 = (bf16[2,64,1332]{2,1,0:T(8,128)(2,1)S(1)}, bf16[2,64,1332]{2,1,0:T(8,128)(2,1)S(1)}, u32[]{:S(2)}, u32[]{:S(2)}) collective-permute-start(bf16[2,64,1332]{2,1,0:T(8,128)(2,1)S(1)} %get-tuple-element.9), channel_id=1, source_target_pairs={{0,2},{1,3},{2,0},{3,1},{4,6},{5,7},{6,4},{7,5},{8,10},{9,11},{10,... | collective-permute-start | bytes 1022984 | tf_op jit(solution)/shard_map/ppermute | solution.py:298
  397.1 16.2 %collective-permute-start.44 = (bf16[2,64,1332]{2,1,0:T(8,128)(2,1)S(1)}, bf16[2,64,1332]{2,1,0:T(8,128)(2,1)S(1)}, u32[]{:S(2)}, u32[]{:S(2)}) collective-permute-start(bf16[2,64,1332]{2,1,0:T(8,128)(2,1)S(1)} %get-tuple-element.8), channel_id=1, source_target_pairs={{0,1},{1,0},{2,3},{3,2},{4,5},{5,4},{6,7},{7,6},{8,9},{9,8},{10,11... | collective-permute-start | bytes 1022984 | tf_op jit(solution)/shard_map/ppermute | solution.py:298
  398.2 33.8 %collective-permute-start.49 = (bf16[4,64,2664]{2,1,0:T(8,128)(2,1)S(1)}, bf16[4,64,2664]{2,1,0:T(8,128)(2,1)S(1)}, u32[]{:S(2)}, u32[]{:S(2)}) collective-permute-start(bf16[4,64,2664]{2,1,0:T(8,128)(2,1)S(1)} %copy-done.17), channel_id=1, source_target_pairs={{8,0},{16,8},{24,16},{28,24},{20,28},{12,20},{4,12},{0,4},{9,1},{1... | collective-permute-start | bytes 4091912 | tf_op jit(solution)/shard_map/ppermute | solution.py:295
  399.9 32.1 %collective-permute-start.48 = (bf16[4,64,2664]{2,1,0:T(8,128)(2,1)}, bf16[4,64,2664]{2,1,0:T(8,128)(2,1)S(1)}, u32[]{:S(2)}, u32[]{:S(2)}) collective-permute-start(bf16[4,64,2664]{2,1,0:T(8,128)(2,1)} %copy-done.21), channel_id=1, source_target_pairs={{8,16},{16,24},{24,28},{28,20},{20,12},{12,4},{4,0},{0,8},{9,17},{... | collective-permute-start | bytes 4091912 | tf_op jit(solution)/shard_map/ppermute | solution.py:295
  414.2 32.6 %collective-permute-start.47 = (bf16[64,1332]{1,0:T(8,128)(2,1)}, bf16[64,1332]{1,0:T(8,128)(2,1)}, u32[]{:S(2)}, u32[]{:S(2)}) collective-permute-start(bf16[64,1332]{1,0:T(8,128)(2,1)} %get-tuple-element.54), channel_id=1, source_target_pairs={{8,4},{16,0},{24,8},{28,16},{20,24},{12,28},{4,20},{0,12},{9,5},{1... | collective-permute-start | bytes 511496 | tf_op jit(solution)/shard_map/ppermute | solution.py:295
  443.3 10.8 %collective-permute-start.52 = (bf16[2,64,1332]{2,1,0:T(8,128)(2,1)S(1)}, bf16[2,64,1332]{2,1,0:T(8,128)(2,1)S(1)}, u32[]{:S(2)}, u32[]{:S(2)}) collective-permute-start(bf16[2,64,1332]{2,1,0:T(8,128)(2,1)S(1)} %get-tuple-element.7), channel_id=1, source_target_pairs={{0,3},{1,2},{2,1},{3,0},{4,7},{5,6},{6,5},{7,4},{8,11},{9,10},{10,... | collective-permute-start | bytes 1022984 | tf_op jit(solution)/shard_map/ppermute | solution.py:298
  443.4 17.0 %collective-permute-start.51 = (bf16[2,64,1332]{2,1,0:T(8,128)(2,1)S(1)}, bf16[2,64,1332]{2,1,0:T(8,128)(2,1)S(1)}, u32[]{:S(2)}, u32[]{:S(2)}) collective-permute-start(bf16[2,64,1332]{2,1,0:T(8,128)(2,1)S(1)} %get-tuple-element.6), channel_id=1, source_target_pairs={{0,2},{1,3},{2,0},{3,1},{4,6},{5,7},{6,4},{7,5},{8,10},{9,11},{10,... | collective-permute-start | bytes 1022984 | tf_op jit(solution)/shard_map/ppermute | solution.py:298
  444.2 18.4 %collective-permute-start.50 = (bf16[2,64,1332]{2,1,0:T(8,128)(2,1)S(1)}, bf16[2,64,1332]{2,1,0:T(8,128)(2,1)S(1)}, u32[]{:S(2)}, u32[]{:S(2)}) collective-permute-start(bf16[2,64,1332]{2,1,0:T(8,128)(2,1)S(1)} %get-tuple-element.5), channel_id=1, source_target_pairs={{0,1},{1,0},{2,3},{3,2},{4,5},{5,4},{6,7},{7,6},{8,9},{9,8},{10,11... | collective-permute-start | bytes 1022984 | tf_op jit(solution)/shard_map/ppermute | solution.py:298
  445.3 19.1 %collective-permute-start.55 = (bf16[4,32,2664]{2,1,0:T(8,128)(2,1)S(1)}, bf16[4,32,2664]{2,1,0:T(8,128)(2,1)S(1)}, u32[]{:S(2)}, u32[]{:S(2)}) collective-permute-start(bf16[4,32,2664]{2,1,0:T(8,128)(2,1)S(1)} %slice.319), channel_id=1, source_target_pairs={{8,0},{16,8},{24,16},{28,24},{20,28},{12,20},{4,12},{0,4},{9,1},{1... | collective-permute-start | bytes 2045960 | tf_op jit(solution)/shard_map/ppermute | solution.py:295
  446.8 18.4 %collective-permute-start.54 = (bf16[4,32,2664]{2,1,0:T(8,128)(2,1)S(1)}, bf16[4,32,2664]{2,1,0:T(8,128)(2,1)S(1)}, u32[]{:S(2)}, u32[]{:S(2)}) collective-permute-start(bf16[4,32,2664]{2,1,0:T(8,128)(2,1)S(1)} %slice.318), channel_id=1, source_target_pairs={{8,16},{16,24},{24,28},{28,20},{20,12},{12,4},{4,0},{0,8},{9,17},{... | collective-permute-start | bytes 2045960 | tf_op jit(solution)/shard_map/ppermute | solution.py:295
  454.1 46.5 %collective-permute-start.62 = (bf16[64,1332]{1,0:T(8,128)(2,1)}, bf16[64,1332]{1,0:T(8,128)(2,1)}, u32[]{:S(2)}, u32[]{:S(2)}) collective-permute-start(bf16[64,1332]{1,0:T(8,128)(2,1)} %get-tuple-element.51), channel_id=1, source_target_pairs={{8,16},{16,24},{24,28},{28,20},{20,12},{12,4},{4,0},{0,8},{9,17},{... | collective-permute-start | bytes 511496 | tf_op jit(solution)/shard_map/ppermute | solution.py:295
  460.4 38.6 %collective-permute-start.61 = (bf16[64,1332]{1,0:T(8,128)(2,1)}, bf16[64,1332]{1,0:T(8,128)(2,1)}, u32[]{:S(2)}, u32[]{:S(2)}) collective-permute-start(bf16[64,1332]{1,0:T(8,128)(2,1)} %get-tuple-element.53), channel_id=1, source_target_pairs={{8,24},{16,28},{24,20},{28,12},{20,4},{12,0},{4,8},{0,16},{9,25},{... | collective-permute-start | bytes 511496 | tf_op jit(solution)/shard_map/ppermute | solution.py:295
  471.0 9.3 %collective-permute-start.57 = (bf16[1,64,1332]{2,1,0:T(8,128)(2,1)S(1)}, bf16[1,64,1332]{2,1,0:T(8,128)(2,1)S(1)}, u32[]{:S(2)}, u32[]{:S(2)}) collective-permute-start(bf16[1,64,1332]{2,1,0:T(8,128)(2,1)S(1)} %get-tuple-element.41), channel_id=1, source_target_pairs={{0,2},{1,3},{2,0},{3,1},{4,6},{5,7},{6,4},{7,5},{8,10},{9,11},{10,... | collective-permute-start | bytes 511496 | tf_op jit(solution)/shard_map/ppermute | solution.py:298
  471.8 11.3 %collective-permute-start.56 = (bf16[1,64,1332]{2,1,0:T(8,128)(2,1)S(1)}, bf16[1,64,1332]{2,1,0:T(8,128)(2,1)S(1)}, u32[]{:S(2)}, u32[]{:S(2)}) collective-permute-start(bf16[1,64,1332]{2,1,0:T(8,128)(2,1)S(1)} %get-tuple-element.39), channel_id=1, source_target_pairs={{0,1},{1,0},{2,3},{3,2},{4,5},{5,4},{6,7},{7,6},{8,9},{9,8},{10,11... | collective-permute-start | bytes 511496 | tf_op jit(solution)/shard_map/ppermute | solution.py:298
  477.8 8.2 %collective-permute-start.53 = (bf16[64,1332]{1,0:T(8,128)(2,1)S(1)}, bf16[64,1332]{1,0:T(8,128)(2,1)S(1)}, u32[]{:S(2)}, u32[]{:S(2)}) collective-permute-start(bf16[64,1332]{1,0:T(8,128)(2,1)S(1)} %get-tuple-element.56), channel_id=1, source_target_pairs={{8,12},{16,4},{24,0},{28,8},{20,16},{12,24},{4,28},{0,20},{9,13},{... | collective-permute-start | bytes 511496 | tf_op jit(solution)/shard_map/ppermute | solution.py:295
  480.3 17.9 %collective-permute-start.60 = (bf16[64,1332]{1,0:T(8,128)(2,1)S(1)}, bf16[64,1332]{1,0:T(8,128)(2,1)S(1)}, u32[]{:S(2)}, u32[]{:S(2)}) collective-permute-start(bf16[64,1332]{1,0:T(8,128)(2,1)S(1)} %get-tuple-element.55), channel_id=1, source_target_pairs={{8,28},{16,20},{24,12},{28,4},{20,0},{12,8},{4,16},{0,24},{9,29},{... | collective-permute-start | bytes 511496 | tf_op jit(solution)/shard_map/ppermute | solution.py:295
  483.2 11.2 %collective-permute-start.59 = (bf16[64,1332]{1,0:T(8,128)(2,1)S(1)}, bf16[64,1332]{1,0:T(8,128)(2,1)S(1)}, u32[]{:S(2)}, u32[]{:S(2)}) collective-permute-start(bf16[64,1332]{1,0:T(8,128)(2,1)S(1)} %fusion.37), channel_id=1, source_target_pairs={{8,20},{16,12},{24,4},{28,0},{20,8},{12,16},{4,24},{0,28},{9,21},{... | collective-permute-start | bytes 511496 | tf_op jit(solution)/shard_map/ppermute | solution.py:295
  576.8 10.2 %collective-permute-start.65 = (bf16[64,2664]{1,0:T(8,128)(2,1)S(1)}, bf16[64,2664]{1,0:T(8,128)(2,1)S(1)}, u32[]{:S(2)}, u32[]{:S(2)}) collective-permute-start(bf16[64,2664]{1,0:T(8,128)(2,1)S(1)} %get-tuple-element.28), channel_id=1, source_target_pairs={{0,3},{1,2},{2,1},{3,0},{4,7},{5,6},{6,5},{7,4},{8,11},{9,10},{10,... | collective-permute-start | bytes 1022984 | tf_op jit(solution)/shard_map/ppermute | solution.py:298
  578.0 16.6 %collective-permute-start.64 = (bf16[64,2664]{1,0:T(8,128)(2,1)S(1)}, bf16[64,2664]{1,0:T(8,128)(2,1)S(1)}, u32[]{:S(2)}, u32[]{:S(2)}) collective-permute-start(bf16[64,2664]{1,0:T(8,128)(2,1)S(1)} %get-tuple-element.29), channel_id=1, source_target_pairs={{0,2},{1,3},{2,0},{3,1},{4,6},{5,7},{6,4},{7,5},{8,10},{9,11},{10,... | collective-permute-start | bytes 1022984 | tf_op jit(solution)/shard_map/ppermute | solution.py:298
  578.5 16.1 %collective-permute-start.63 = (bf16[64,2664]{1,0:T(8,128)(2,1)S(1)}, bf16[64,2664]{1,0:T(8,128)(2,1)S(1)}, u32[]{:S(2)}, u32[]{:S(2)}) collective-permute-start(bf16[64,2664]{1,0:T(8,128)(2,1)S(1)} %get-tuple-element.30), channel_id=1, source_target_pairs={{0,1},{1,0},{2,3},{3,2},{4,5},{5,4},{6,7},{7,6},{8,9},{9,8},{10,11... | collective-permute-start | bytes 1022984 | tf_op jit(solution)/shard_map/ppermute | solution.py:298
  (31 other events, 124.8 us)
